TPU v7x, 128 devices: a whole 4x4x4 slice. The times are simulated.
128 devices in a mesh: ctx: 32 (over z, x, core), exp: 4 (over y).
Axes of the slice: x: 4, y: 4, z: 4, core: 2. Of those that a mesh axis runs over, the one named last changes fastest.
Arguments:
- queries: bfloat16 [4096, 6144], P('ctx', 'exp'), may hold values from -6 to 6
- keys: bfloat16 [4096, 6144], P('ctx', 'exp'), may hold values from -6 to 6
- values: bfloat16 [4096, 6144], P('ctx', 'exp'), may hold values from -6 to 6
- out_grad: bfloat16 [4096, 6144], P('ctx', 'exp'), may hold values from -6 to 6
- up_weight: bfloat16 [32, 6144, 2304], P('ctx', 'exp'), may hold values from -0.078125 to 0.078125
- down_weight: bfloat16 [32, 2304, 6144], P('ctx', None, 'exp'), may hold values from -0.09375 to 0.09375
- decay_rates: float32 [48], P('exp'), may hold values from 2.4414063e-05 to 0.0333333333
- routes: int32 [4096, 2], P('ctx'), may hold values from 0 to 15, all different within a row; in each aligned block of 128 rows (0 to 127, 128 to 255, ...) at most 18 rows name the same one
- gate_weights: float32 [4096, 2], P('ctx'), may hold values from 0.1 to 1
Outputs:
- query_grad: bfloat16 [4096, 6144], P('ctx', 'exp')
- key_grad: bfloat16 [4096, 6144], P('ctx', 'exp')
- value_grad: bfloat16 [4096, 6144], P('ctx', 'exp')
Inputs may be any that keep to these rules, and one draw needn't show every extreme that they name: `routes`: in each aligned block of 128 tokens a token's two experts differ and no expert is named by more than 18 tokens; in every draw some expert is named by exactly 18 tokens of some block.
All inputs are finite; a program needn't handle non-finite values.
Results may differ from a plain program's by a relative error of at most 0.0117.
Values may be sent and summed in bfloat16 or wider, within the bound.
A program may use at most 128 MiB of HBM per device.

v0:
```python
import jax
import jax.numpy as jnp
from jax import lax
from jax.sharding import PartitionSpec as P

DH = 128


HIGHEST = lax.Precision.HIGHEST


def from_behind(array, axis, by):
    peers = lax.axis_size(axis)
    pairs = [(i, i + by) for i in range(peers) if 0 <= i + by < peers]
    return lax.ppermute(array, axis, pairs)


def silu_slope(value):
    sigma = jax.nn.sigmoid(value)
    return sigma * (1.0 + value * (1.0 - sigma))


def decay_tables(rates, block_len):
    offsets = jnp.arange(block_len).astype(jnp.float32)
    distance = offsets[:, None] - offsets[None, :]
    within = jnp.where(
        distance[None] >= 0.0,
        jnp.exp(-rates[:, None, None] * jnp.maximum(distance, 0.0)[None]),
        0.0,
    )
    start_pow = jnp.exp(-rates[None, :] * offsets[:, None])
    end_pow = jnp.exp(-rates[None, :] * (block_len - offsets)[:, None])
    last_pow = jnp.exp(-rates[None, :] * (block_len - 1.0 - offsets)[:, None])
    next_pow = jnp.exp(-rates[None, :] * (offsets + 1.0)[:, None])
    whole_pow = jnp.exp(-rates * block_len)
    return (within, start_pow, end_pow, last_pow, next_pow, whole_pow)


def slot_tables(route_block, gate_block, experts, capacity):
    flat = route_block.reshape(-1)
    hits = (flat[:, None] == jnp.arange(experts, dtype=jnp.int32)[None, :]).astype(jnp.int32)
    before = jnp.cumsum(hits, axis=0) - hits
    placed = jnp.sum(before * hits, axis=1)
    target = flat * capacity + placed
    match = (target[None, :] == jnp.arange(experts * capacity, dtype=jnp.int32)[:, None]).astype(
        jnp.float32
    )
    match = match.reshape(experts * capacity, route_block.shape[0], route_block.shape[1])
    return (jnp.sum(match, axis=2), jnp.sum(match * gate_block[None], axis=2))


def forward_states(factor, local):

    def forward_advance(step, incoming):
        return from_behind(factor * incoming + local, "ctx", 1)

    return lax.fori_loop(0, lax.axis_size("ctx") - 1, forward_advance, jnp.zeros_like(local))


def reverse_states(factor, local):

    def reverse_advance(step, incoming):
        return from_behind(factor * incoming + local, "ctx", -1)

    return lax.fori_loop(0, lax.axis_size("ctx") - 1, reverse_advance, jnp.zeros_like(local))


def contract_last(left, right):
    return lax.dot_general(
        left, right, (((1,), (1,)), ((), ())), preferred_element_type=jnp.float32
    )


def on_device(
    queries, keys, values, out_grad, up_weight, down_weight, decay_rates, routes, gate_weights
):
    block_len = queries.shape[0]
    group = queries.shape[1]
    heads = group // DH
    scale = 1.0 / DH
    within, start_pow, end_pow, last_pow, next_pow, whole_pow = decay_tables(decay_rates, block_len)
    factor = whole_pow[:, None, None]
    query_heads = queries.reshape(block_len, heads, DH)
    key_heads = keys.reshape(block_len, heads, DH)
    value_heads = values.reshape(block_len, heads, DH)
    query_wide = query_heads.astype(jnp.float32)
    key_wide = key_heads.astype(jnp.float32)
    value_wide = value_heads.astype(jnp.float32)
    scores = jnp.einsum("ihd,jhd->hij", query_heads, key_heads, preferred_element_type=jnp.float32)
    weights = (scale * scores * within).astype(jnp.bfloat16)
    intra = jnp.einsum("hij,jhd->ihd", weights, value_heads, preferred_element_type=jnp.float32)
    key_local = jnp.einsum(
        "ihd,ihe->hde", key_wide * end_pow[:, :, None], value_wide, precision=HIGHEST
    )
    entering = forward_states(factor, key_local)
    inter = (
        scale
        * start_pow[:, :, None]
        * jnp.einsum("ihd,hde->ihe", query_wide, entering, precision=HIGHEST)
    )
    attn_out = (intra + inter).astype(jnp.bfloat16).reshape(block_len, group)
    experts = lax.axis_size("ctx") // 2
    capacity = block_len * 9 // (4 * experts)
    choose, weigh = slot_tables(routes, gate_weights, experts, capacity)
    choose_half = choose.astype(jnp.bfloat16)
    send_in = jnp.dot(choose_half, attn_out, preferred_element_type=jnp.float32).astype(
        jnp.bfloat16
    )
    send_grad = jnp.dot(choose_half, out_grad, preferred_element_type=jnp.float32).astype(
        jnp.bfloat16
    )

    def doubled(array):
        spread = jnp.broadcast_to(
            array.reshape(experts, 1, capacity, group), (experts, 2, capacity, group)
        )
        return spread.reshape(2 * experts, capacity, group)

    got_in, got_grad = (
        lax.all_to_all(doubled(send_in), "ctx", split_axis=0, concat_axis=0, tiled=True),
        lax.all_to_all(doubled(send_grad), "ctx", split_axis=0, concat_axis=0, tiled=True),
    )
    in_rows = got_in.reshape(-1, group)
    grad_rows = got_grad.reshape(-1, group)
    up_local = up_weight[0]
    down_local = down_weight[0]
    pre_part = jnp.dot(in_rows, up_local, preferred_element_type=jnp.float32)
    grad_part = contract_last(grad_rows, down_local)
    pre, hidden_grad = (
        lax.psum(pre_part.astype(jnp.bfloat16), "exp").astype(jnp.float32),
        lax.psum(grad_part.astype(jnp.bfloat16), "exp").astype(jnp.float32),
    )
    slope = (hidden_grad * silu_slope(pre)).astype(jnp.bfloat16)
    back = contract_last(slope, up_local)
    back_half = back.astype(jnp.bfloat16).reshape(2 * experts, capacity, group)
    home = lax.all_to_all(back_half, "ctx", split_axis=0, concat_axis=0, tiled=True)
    summed = jnp.sum(home.astype(jnp.float32).reshape(experts, 2, capacity, group), axis=1)
    summed = summed.reshape(experts * capacity, group)
    moe_grad = lax.dot_general(
        weigh,
        summed,
        (((0,), (0,)), ((), ())),
        precision=HIGHEST,
        preferred_element_type=jnp.float32,
    )
    grad_out = (out_grad.astype(jnp.float32) + moe_grad).astype(jnp.bfloat16)
    grad_heads = grad_out.reshape(block_len, heads, DH)
    grad_wide = grad_heads.astype(jnp.float32)
    query_local = jnp.einsum(
        "ihd,ihe->hde", query_wide * next_pow[:, :, None], grad_wide, precision=HIGHEST
    )
    leaving = reverse_states(factor, query_local)
    dscores = jnp.einsum(
        "ihd,jhd->hij", grad_heads, value_heads, preferred_element_type=jnp.float32
    )
    dweights = (scale * dscores * within).astype(jnp.bfloat16)
    query_g = jnp.einsum("hij,jhd->ihd", dweights, key_heads, preferred_element_type=jnp.float32)
    query_g = query_g + scale * start_pow[:, :, None] * jnp.einsum(
        "ihe,hde->ihd", grad_wide, entering, precision=HIGHEST
    )
    key_g = jnp.einsum("hij,ihd->jhd", dweights, query_heads, preferred_element_type=jnp.float32)
    key_g = key_g + scale * last_pow[:, :, None] * jnp.einsum(
        "jhe,hde->jhd", value_wide, leaving, precision=HIGHEST
    )
    value_g = jnp.einsum("hij,ihd->jhd", weights, grad_heads, preferred_element_type=jnp.float32)
    value_g = value_g + scale * last_pow[:, :, None] * jnp.einsum(
        "jhd,hde->jhe", key_wide, leaving, precision=HIGHEST
    )
    return (
        query_g.astype(jnp.bfloat16).reshape(block_len, group),
        key_g.astype(jnp.bfloat16).reshape(block_len, group),
        value_g.astype(jnp.bfloat16).reshape(block_len, group),
    )


def solution(mesh):
    placed = (
        P("ctx", "exp"),
        P("ctx", "exp"),
        P("ctx", "exp"),
        P("ctx", "exp"),
        P("ctx", "exp", None),
        P("ctx", None, "exp"),
        P("exp"),
        P("ctx", None),
        P("ctx", None),
    )
    return jax.shard_map(
        on_device,
        mesh=mesh,
        in_specs=placed,
        out_specs=(P("ctx", "exp"), P("ctx", "exp"), P("ctx", "exp")),
        check_vma=False,
    )
```

profile of v0, /device:TPU:7, one launch (start us, length us, event | category | flops | bytes accessed | tf_op | source)
XLA Modules:
  0.0 1302.0 jit_solution(14958533447624604293)
XLA Ops:
  19.1 500.6 %while.20 = (s32[]{:T(128)}, f32[12,128,128]{2,1,0:T(8,128)S(1)}, f32[12,1,1]{0,2,1:T(1,128)}, f32[12,128,128]{2,1,0:T(8,128)S(1)}, s32[]{:T(128)}) while((s32[]{:T(128)}, f32[12,128,128]{2,1,0:T(8,128)S(1)}, f32[12,1,1]{0,2,1:T(1,128)}, f32[12,128,128]{2,1,0:T(8,128)S(1)}, s32[]{:T(128)}) %tuple.45), condition=%wide.region_7.8_spmd, body=%wide.region_6.7_spmd.sunk | while | flops 393218 | bytes 5505173 | solution.py:57
  538.2 25.6 %all-to-all-done.1 = bf16[32,18,1536]{2,1,0:T(8,128)(2,1)S(1)} async-done(((bf16[32,18,1536]{2,1,0:T(8,128)(2,1)}), bf16[32,18,1536]{2,1,0:T(8,128)(2,1)S(1)}, u32[]{:S(2)}, u32[]{:S(2)}) %all-to-all-start.1) | async-done | bytes 1769504 | tf_op jit(solution)/shard_map/all_to_all | solution.py:120
  585.4 19.2 %all-to-all-done = bf16[32,18,1536]{2,1,0:T(8,128)(2,1)} async-done(((bf16[32,18,1536]{2,1,0:T(8,128)(2,1)}), bf16[32,18,1536]{2,1,0:T(8,128)(2,1)}, u32[]{:S(2)}, u32[]{:S(2)}) %all-to-all-start) | async-done | bytes 1769504 | tf_op jit(solution)/shard_map/all_to_all | solution.py:121
  615.8 110.2 %all-reduce.3.cloned.1.call-done = (bf16[576,2304]{1,0:T(8,128)(2,1)}, bf16[576,2304]{1,0:T(8,128)(2,1)}) async-done(((bf16[576,2304]{1,0:T(8,128)(2,1)}, bf16[576,2304]{1,0:T(8,128)(2,1)}), (bf16[576,2304]{1,0:T(8,128)(2,1)}, bf16[576,2304]{1,0:T(8,128)(2,1)})) %all-reduce.3.cloned.1.call-update) | async-done | bytes 5308432 | tf_op jit(solution)/shard_map/psum | solution.py:130
  739.5 37.7 %all_to_all.15 = bf16[32,18,1536]{2,1,0:T(8,128)(2,1)S(1)} all-to-all(bf16[32,18,1536]{2,1,0:T(8,128)(2,1)S(1)} %reshape.285), channel_id=1, replica_groups=mesh['ctx'=32,'exp'=4] {'ctx'}, dimensions={0} | all-to-all | bytes 3538944 | tf_op jit(solution)/shard_map/all_to_all | solution.py:136
  786.1 503.1 %while.21 = (s32[]{:T(128)}, f32[12,128,128]{2,1,0:T(8,128)S(1)}, f32[12,1,1]{0,2,1:T(1,128)}, f32[12,128,128]{2,1,0:T(8,128)S(1)}, s32[]{:T(128)}) while((s32[]{:T(128)}, f32[12,128,128]{2,1,0:T(8,128)S(1)}, f32[12,1,1]{0,2,1:T(1,128)}, f32[12,128,128]{2,1,0:T(8,128)S(1)}, s32[]{:T(128)}) %tuple.48), condition=%wide.region_11.12_spmd, body=%wide.region_10.11_spmd.sunk | while | flops 393218 | bytes 5505173 | solution.py:65
  805.1 13.5 %collective-permute-done.1 = f32[12,128,128]{2,1,0:T(8,128)S(1)} collective-permute-done((f32[12,128,128]{2,1,0:T(8,128)S(1)}, f32[12,128,128]{2,1,0:T(8,128)S(1)}, u32[]{:S(2)}, u32[]{:S(2)}) %collective-permute-start.1) | collective-permute-done | bytes 786464 | tf_op jit(solution)/shard_map/while/body/eval_jaxpr/ppermute | solution.py:15
  821.3 13.5 %collective-permute-done.1 = f32[12,128,128]{2,1,0:T(8,128)S(1)} collective-permute-done((f32[12,128,128]{2,1,0:T(8,128)S(1)}, f32[12,128,128]{2,1,0:T(8,128)S(1)}, u32[]{:S(2)}, u32[]{:S(2)}) %collective-permute-start.1) | collective-permute-done | bytes 786464 | tf_op jit(solution)/shard_map/while/body/eval_jaxpr/ppermute | solution.py:15
  837.5 13.5 %collective-permute-done.1 = f32[12,128,128]{2,1,0:T(8,128)S(1)} collective-permute-done((f32[12,128,128]{2,1,0:T(8,128)S(1)}, f32[12,128,128]{2,1,0:T(8,128)S(1)}, u32[]{:S(2)}, u32[]{:S(2)}) %collective-permute-start.1) | collective-permute-done | bytes 786464 | tf_op jit(solution)/shard_map/while/body/eval_jaxpr/ppermute | solution.py:15
  853.7 13.5 %collective-permute-done.1 = f32[12,128,128]{2,1,0:T(8,128)S(1)} collective-permute-done((f32[12,128,128]{2,1,0:T(8,128)S(1)}, f32[12,128,128]{2,1,0:T(8,128)S(1)}, u32[]{:S(2)}, u32[]{:S(2)}) %collective-permute-start.1) | collective-permute-done | bytes 786464 | tf_op jit(solution)/shard_map/while/body/eval_jaxpr/ppermute | solution.py:15
  870.0 13.5 %collective-permute-done.1 = f32[12,128,128]{2,1,0:T(8,128)S(1)} collective-permute-done((f32[12,128,128]{2,1,0:T(8,128)S(1)}, f32[12,128,128]{2,1,0:T(8,128)S(1)}, u32[]{:S(2)}, u32[]{:S(2)}) %collective-permute-start.1) | collective-permute-done | bytes 786464 | tf_op jit(solution)/shard_map/while/body/eval_jaxpr/ppermute | solution.py:15
  886.2 13.5 %collective-permute-done.1 = f32[12,128,128]{2,1,0:T(8,128)S(1)} collective-permute-done((f32[12,128,128]{2,1,0:T(8,128)S(1)}, f32[12,128,128]{2,1,0:T(8,128)S(1)}, u32[]{:S(2)}, u32[]{:S(2)}) %collective-permute-start.1) | collective-permute-done | bytes 786464 | tf_op jit(solution)/shard_map/while/body/eval_jaxpr/ppermute | solution.py:15
  902.4 13.5 %collective-permute-done.1 = f32[12,128,128]{2,1,0:T(8,128)S(1)} collective-permute-done((f32[12,128,128]{2,1,0:T(8,128)S(1)}, f32[12,128,128]{2,1,0:T(8,128)S(1)}, u32[]{:S(2)}, u32[]{:S(2)}) %collective-permute-start.1) | collective-permute-done | bytes 786464 | tf_op jit(solution)/shard_map/while/body/eval_jaxpr/ppermute | solution.py:15
  918.6 13.5 %collective-permute-done.1 = f32[12,128,128]{2,1,0:T(8,128)S(1)} collective-permute-done((f32[12,128,128]{2,1,0:T(8,128)S(1)}, f32[12,128,128]{2,1,0:T(8,128)S(1)}, u32[]{:S(2)}, u32[]{:S(2)}) %collective-permute-start.1) | collective-permute-done | bytes 786464 | tf_op jit(solution)/shard_map/while/body/eval_jaxpr/ppermute | solution.py:15
  934.9 13.5 %collective-permute-done.1 = f32[12,128,128]{2,1,0:T(8,128)S(1)} collective-permute-done((f32[12,128,128]{2,1,0:T(8,128)S(1)}, f32[12,128,128]{2,1,0:T(8,128)S(1)}, u32[]{:S(2)}, u32[]{:S(2)}) %collective-permute-start.1) | collective-permute-done | bytes 786464 | tf_op jit(solution)/shard_map/while/body/eval_jaxpr/ppermute | solution.py:15
  951.1 13.5 %collective-permute-done.1 = f32[12,128,128]{2,1,0:T(8,128)S(1)} collective-permute-done((f32[12,128,128]{2,1,0:T(8,128)S(1)}, f32[12,128,128]{2,1,0:T(8,128)S(1)}, u32[]{:S(2)}, u32[]{:S(2)}) %collective-permute-start.1) | collective-permute-done | bytes 786464 | tf_op jit(solution)/shard_map/while/body/eval_jaxpr/ppermute | solution.py:15
  967.3 13.5 %collective-permute-done.1 = f32[12,128,128]{2,1,0:T(8,128)S(1)} collective-permute-done((f32[12,128,128]{2,1,0:T(8,128)S(1)}, f32[12,128,128]{2,1,0:T(8,128)S(1)}, u32[]{:S(2)}, u32[]{:S(2)}) %collective-permute-start.1) | collective-permute-done | bytes 786464 | tf_op jit(solution)/shard_map/while/body/eval_jaxpr/ppermute | solution.py:15
  983.6 13.5 %collective-permute-done.1 = f32[12,128,128]{2,1,0:T(8,128)S(1)} collective-permute-done((f32[12,128,128]{2,1,0:T(8,128)S(1)}, f32[12,128,128]{2,1,0:T(8,128)S(1)}, u32[]{:S(2)}, u32[]{:S(2)}) %collective-permute-start.1) | collective-permute-done | bytes 786464 | tf_op jit(solution)/shard_map/while/body/eval_jaxpr/ppermute | solution.py:15
  999.8 13.5 %collective-permute-done.1 = f32[12,128,128]{2,1,0:T(8,128)S(1)} collective-permute-done((f32[12,128,128]{2,1,0:T(8,128)S(1)}, f32[12,128,128]{2,1,0:T(8,128)S(1)}, u32[]{:S(2)}, u32[]{:S(2)}) %collective-permute-start.1) | collective-permute-done | bytes 786464 | tf_op jit(solution)/shard_map/while/body/eval_jaxpr/ppermute | solution.py:15
  1032.2 13.5 %collective-permute-done.1 = f32[12,128,128]{2,1,0:T(8,128)S(1)} collective-permute-done((f32[12,128,128]{2,1,0:T(8,128)S(1)}, f32[12,128,128]{2,1,0:T(8,128)S(1)}, u32[]{:S(2)}, u32[]{:S(2)}) %collective-permute-start.1) | collective-permute-done | bytes 786464 | tf_op jit(solution)/shard_map/while/body/eval_jaxpr/ppermute | solution.py:15
  1048.5 13.5 %collective-permute-done.1 = f32[12,128,128]{2,1,0:T(8,128)S(1)} collective-permute-done((f32[12,128,128]{2,1,0:T(8,128)S(1)}, f32[12,128,128]{2,1,0:T(8,128)S(1)}, u32[]{:S(2)}, u32[]{:S(2)}) %collective-permute-start.1) | collective-permute-done | bytes 786464 | tf_op jit(solution)/shard_map/while/body/eval_jaxpr/ppermute | solution.py:15
  1064.7 13.5 %collective-permute-done.1 = f32[12,128,128]{2,1,0:T(8,128)S(1)} collective-permute-done((f32[12,128,128]{2,1,0:T(8,128)S(1)}, f32[12,128,128]{2,1,0:T(8,128)S(1)}, u32[]{:S(2)}, u32[]{:S(2)}) %collective-permute-start.1) | collective-permute-done | bytes 786464 | tf_op jit(solution)/shard_map/while/body/eval_jaxpr/ppermute | solution.py:15
  1097.2 13.5 %collective-permute-done.1 = f32[12,128,128]{2,1,0:T(8,128)S(1)} collective-permute-done((f32[12,128,128]{2,1,0:T(8,128)S(1)}, f32[12,128,128]{2,1,0:T(8,128)S(1)}, u32[]{:S(2)}, u32[]{:S(2)}) %collective-permute-start.1) | collective-permute-done | bytes 786464 | tf_op jit(solution)/shard_map/while/body/eval_jaxpr/ppermute | solution.py:15
  1113.4 13.5 %collective-permute-done.1 = f32[12,128,128]{2,1,0:T(8,128)S(1)} collective-permute-done((f32[12,128,128]{2,1,0:T(8,128)S(1)}, f32[12,128,128]{2,1,0:T(8,128)S(1)}, u32[]{:S(2)}, u32[]{:S(2)}) %collective-permute-start.1) | collective-permute-done | bytes 786464 | tf_op jit(solution)/shard_map/while/body/eval_jaxpr/ppermute | solution.py:15
  1129.6 13.5 %collective-permute-done.1 = f32[12,128,128]{2,1,0:T(8,128)S(1)} collective-permute-done((f32[12,128,128]{2,1,0:T(8,128)S(1)}, f32[12,128,128]{2,1,0:T(8,128)S(1)}, u32[]{:S(2)}, u32[]{:S(2)}) %collective-permute-start.1) | collective-permute-done | bytes 786464 | tf_op jit(solution)/shard_map/while/body/eval_jaxpr/ppermute | solution.py:15
  1162.1 13.5 %collective-permute-done.1 = f32[12,128,128]{2,1,0:T(8,128)S(1)} collective-permute-done((f32[12,128,128]{2,1,0:T(8,128)S(1)}, f32[12,128,128]{2,1,0:T(8,128)S(1)}, u32[]{:S(2)}, u32[]{:S(2)}) %collective-permute-start.1) | collective-permute-done | bytes 786464 | tf_op jit(solution)/shard_map/while/body/eval_jaxpr/ppermute | solution.py:15
  1178.3 13.5 %collective-permute-done.1 = f32[12,128,128]{2,1,0:T(8,128)S(1)} collective-permute-done((f32[12,128,128]{2,1,0:T(8,128)S(1)}, f32[12,128,128]{2,1,0:T(8,128)S(1)}, u32[]{:S(2)}, u32[]{:S(2)}) %collective-permute-start.1) | collective-permute-done | bytes 786464 | tf_op jit(solution)/shard_map/while/body/eval_jaxpr/ppermute | solution.py:15
  1194.5 13.5 %collective-permute-done.1 = f32[12,128,128]{2,1,0:T(8,128)S(1)} collective-permute-done((f32[12,128,128]{2,1,0:T(8,128)S(1)}, f32[12,128,128]{2,1,0:T(8,128)S(1)}, u32[]{:S(2)}, u32[]{:S(2)}) %collective-permute-start.1) | collective-permute-done | bytes 786464 | tf_op jit(solution)/shard_map/while/body/eval_jaxpr/ppermute | solution.py:15
  1210.8 13.5 %collective-permute-done.1 = f32[12,128,128]{2,1,0:T(8,128)S(1)} collective-permute-done((f32[12,128,128]{2,1,0:T(8,128)S(1)}, f32[12,128,128]{2,1,0:T(8,128)S(1)}, u32[]{:S(2)}, u32[]{:S(2)}) %collective-permute-start.1) | collective-permute-done | bytes 786464 | tf_op jit(solution)/shard_map/while/body/eval_jaxpr/ppermute | solution.py:15
  1227.0 13.5 %collective-permute-done.1 = f32[12,128,128]{2,1,0:T(8,128)S(1)} collective-permute-done((f32[12,128,128]{2,1,0:T(8,128)S(1)}, f32[12,128,128]{2,1,0:T(8,128)S(1)}, u32[]{:S(2)}, u32[]{:S(2)}) %collective-permute-start.1) | collective-permute-done | bytes 786464 | tf_op jit(solution)/shard_map/while/body/eval_jaxpr/ppermute | solution.py:15
  1243.2 13.5 %collective-permute-done.1 = f32[12,128,128]{2,1,0:T(8,128)S(1)} collective-permute-done((f32[12,128,128]{2,1,0:T(8,128)S(1)}, f32[12,128,128]{2,1,0:T(8,128)S(1)}, u32[]{:S(2)}, u32[]{:S(2)}) %collective-permute-start.1) | collective-permute-done | bytes 786464 | tf_op jit(solution)/shard_map/while/body/eval_jaxpr/ppermute | solution.py:15
  1275.7 13.5 %collective-permute-done.1 = f32[12,128,128]{2,1,0:T(8,128)S(1)} collective-permute-done((f32[12,128,128]{2,1,0:T(8,128)S(1)}, f32[12,128,128]{2,1,0:T(8,128)S(1)}, u32[]{:S(2)}, u32[]{:S(2)}) %collective-permute-start.1) | collective-permute-done | bytes 786464 | tf_op jit(solution)/shard_map/while/body/eval_jaxpr/ppermute | solution.py:15
  (254 shorter events, 743.1 us)
Async XLA Ops:
  33.7 15.4 %collective-permute-start = (f32[12,128,128]{2,1,0:T(8,128)S(1)}, f32[12,128,128]{2,1,0:T(8,128)S(1)}, u32[]{:S(2)}, u32[]{:S(2)}) collective-permute-start(f32[12,128,128]{2,1,0:T(8,128)S(1)} %multiply_add_fusion.5), channel_id=1, source_target_pairs={{0,4},{4,8},{8,12},{12,16},{16,20},{20,24},{24,28},{28,32},{32,36}... | collective-permute-start | bytes 2359304 | tf_op jit(solution)/shard_map/while/body/eval_jaxpr/ppermute | solution.py:15
  49.9 15.4 %collective-permute-start = (f32[12,128,128]{2,1,0:T(8,128)S(1)}, f32[12,128,128]{2,1,0:T(8,128)S(1)}, u32[]{:S(2)}, u32[]{:S(2)}) collective-permute-start(f32[12,128,128]{2,1,0:T(8,128)S(1)} %multiply_add_fusion.5), channel_id=1, source_target_pairs={{0,4},{4,8},{8,12},{12,16},{16,20},{20,24},{24,28},{28,32},{32,36}... | collective-permute-start | bytes 2359304 | tf_op jit(solution)/shard_map/while/body/eval_jaxpr/ppermute | solution.py:15
  66.1 15.4 %collective-permute-start = (f32[12,128,128]{2,1,0:T(8,128)S(1)}, f32[12,128,128]{2,1,0:T(8,128)S(1)}, u32[]{:S(2)}, u32[]{:S(2)}) collective-permute-start(f32[12,128,128]{2,1,0:T(8,128)S(1)} %multiply_add_fusion.5), channel_id=1, source_target_pairs={{0,4},{4,8},{8,12},{12,16},{16,20},{20,24},{24,28},{28,32},{32,36}... | collective-permute-start | bytes 2359304 | tf_op jit(solution)/shard_map/while/body/eval_jaxpr/ppermute | solution.py:15
  82.4 15.4 %collective-permute-start = (f32[12,128,128]{2,1,0:T(8,128)S(1)}, f32[12,128,128]{2,1,0:T(8,128)S(1)}, u32[]{:S(2)}, u32[]{:S(2)}) collective-permute-start(f32[12,128,128]{2,1,0:T(8,128)S(1)} %multiply_add_fusion.5), channel_id=1, source_target_pairs={{0,4},{4,8},{8,12},{12,16},{16,20},{20,24},{24,28},{28,32},{32,36}... | collective-permute-start | bytes 2359304 | tf_op jit(solution)/shard_map/while/body/eval_jaxpr/ppermute | solution.py:15
  98.6 15.4 %collective-permute-start = (f32[12,128,128]{2,1,0:T(8,128)S(1)}, f32[12,128,128]{2,1,0:T(8,128)S(1)}, u32[]{:S(2)}, u32[]{:S(2)}) collective-permute-start(f32[12,128,128]{2,1,0:T(8,128)S(1)} %multiply_add_fusion.5), channel_id=1, source_target_pairs={{0,4},{4,8},{8,12},{12,16},{16,20},{20,24},{24,28},{28,32},{32,36}... | collective-permute-start | bytes 2359304 | tf_op jit(solution)/shard_map/while/body/eval_jaxpr/ppermute | solution.py:15
  114.8 15.4 %collective-permute-start = (f32[12,128,128]{2,1,0:T(8,128)S(1)}, f32[12,128,128]{2,1,0:T(8,128)S(1)}, u32[]{:S(2)}, u32[]{:S(2)}) collective-permute-start(f32[12,128,128]{2,1,0:T(8,128)S(1)} %multiply_add_fusion.5), channel_id=1, source_target_pairs={{0,4},{4,8},{8,12},{12,16},{16,20},{20,24},{24,28},{28,32},{32,36}... | collective-permute-start | bytes 2359304 | tf_op jit(solution)/shard_map/while/body/eval_jaxpr/ppermute | solution.py:15
  131.0 15.4 %collective-permute-start = (f32[12,128,128]{2,1,0:T(8,128)S(1)}, f32[12,128,128]{2,1,0:T(8,128)S(1)}, u32[]{:S(2)}, u32[]{:S(2)}) collective-permute-start(f32[12,128,128]{2,1,0:T(8,128)S(1)} %multiply_add_fusion.5), channel_id=1, source_target_pairs={{0,4},{4,8},{8,12},{12,16},{16,20},{20,24},{24,28},{28,32},{32,36}... | collective-permute-start | bytes 2359304 | tf_op jit(solution)/shard_map/while/body/eval_jaxpr/ppermute | solution.py:15
  147.3 15.4 %collective-permute-start = (f32[12,128,128]{2,1,0:T(8,128)S(1)}, f32[12,128,128]{2,1,0:T(8,128)S(1)}, u32[]{:S(2)}, u32[]{:S(2)}) collective-permute-start(f32[12,128,128]{2,1,0:T(8,128)S(1)} %multiply_add_fusion.5), channel_id=1, source_target_pairs={{0,4},{4,8},{8,12},{12,16},{16,20},{20,24},{24,28},{28,32},{32,36}... | collective-permute-start | bytes 2359304 | tf_op jit(solution)/shard_map/while/body/eval_jaxpr/ppermute | solution.py:15
  163.5 15.4 %collective-permute-start = (f32[12,128,128]{2,1,0:T(8,128)S(1)}, f32[12,128,128]{2,1,0:T(8,128)S(1)}, u32[]{:S(2)}, u32[]{:S(2)}) collective-permute-start(f32[12,128,128]{2,1,0:T(8,128)S(1)} %multiply_add_fusion.5), channel_id=1, source_target_pairs={{0,4},{4,8},{8,12},{12,16},{16,20},{20,24},{24,28},{28,32},{32,36}... | collective-permute-start | bytes 2359304 | tf_op jit(solution)/shard_map/while/body/eval_jaxpr/ppermute | solution.py:15
  179.7 15.4 %collective-permute-start = (f32[12,128,128]{2,1,0:T(8,128)S(1)}, f32[12,128,128]{2,1,0:T(8,128)S(1)}, u32[]{:S(2)}, u32[]{:S(2)}) collective-permute-start(f32[12,128,128]{2,1,0:T(8,128)S(1)} %multiply_add_fusion.5), channel_id=1, source_target_pairs={{0,4},{4,8},{8,12},{12,16},{16,20},{20,24},{24,28},{28,32},{32,36}... | collective-permute-start | bytes 2359304 | tf_op jit(solution)/shard_map/while/body/eval_jaxpr/ppermute | solution.py:15
  195.9 15.4 %collective-permute-start = (f32[12,128,128]{2,1,0:T(8,128)S(1)}, f32[12,128,128]{2,1,0:T(8,128)S(1)}, u32[]{:S(2)}, u32[]{:S(2)}) collective-permute-start(f32[12,128,128]{2,1,0:T(8,128)S(1)} %multiply_add_fusion.5), channel_id=1, source_target_pairs={{0,4},{4,8},{8,12},{12,16},{16,20},{20,24},{24,28},{28,32},{32,36}... | collective-permute-start | bytes 2359304 | tf_op jit(solution)/shard_map/while/body/eval_jaxpr/ppermute | solution.py:15
  212.2 15.4 %collective-permute-start = (f32[12,128,128]{2,1,0:T(8,128)S(1)}, f32[12,128,128]{2,1,0:T(8,128)S(1)}, u32[]{:S(2)}, u32[]{:S(2)}) collective-permute-start(f32[12,128,128]{2,1,0:T(8,128)S(1)} %multiply_add_fusion.5), channel_id=1, source_target_pairs={{0,4},{4,8},{8,12},{12,16},{16,20},{20,24},{24,28},{28,32},{32,36}... | collective-permute-start | bytes 2359304 | tf_op jit(solution)/shard_map/while/body/eval_jaxpr/ppermute | solution.py:15
  228.4 15.4 %collective-permute-start = (f32[12,128,128]{2,1,0:T(8,128)S(1)}, f32[12,128,128]{2,1,0:T(8,128)S(1)}, u32[]{:S(2)}, u32[]{:S(2)}) collective-permute-start(f32[12,128,128]{2,1,0:T(8,128)S(1)} %multiply_add_fusion.5), channel_id=1, source_target_pairs={{0,4},{4,8},{8,12},{12,16},{16,20},{20,24},{24,28},{28,32},{32,36}... | collective-permute-start | bytes 2359304 | tf_op jit(solution)/shard_map/while/body/eval_jaxpr/ppermute | solution.py:15
  244.6 15.4 %collective-permute-start = (f32[12,128,128]{2,1,0:T(8,128)S(1)}, f32[12,128,128]{2,1,0:T(8,128)S(1)}, u32[]{:S(2)}, u32[]{:S(2)}) collective-permute-start(f32[12,128,128]{2,1,0:T(8,128)S(1)} %multiply_add_fusion.5), channel_id=1, source_target_pairs={{0,4},{4,8},{8,12},{12,16},{16,20},{20,24},{24,28},{28,32},{32,36}... | collective-permute-start | bytes 2359304 | tf_op jit(solution)/shard_map/while/body/eval_jaxpr/ppermute | solution.py:15
  260.9 15.4 %collective-permute-start = (f32[12,128,128]{2,1,0:T(8,128)S(1)}, f32[12,128,128]{2,1,0:T(8,128)S(1)}, u32[]{:S(2)}, u32[]{:S(2)}) collective-permute-start(f32[12,128,128]{2,1,0:T(8,128)S(1)} %multiply_add_fusion.5), channel_id=1, source_target_pairs={{0,4},{4,8},{8,12},{12,16},{16,20},{20,24},{24,28},{28,32},{32,36}... | collective-permute-start | bytes 2359304 | tf_op jit(solution)/shard_map/while/body/eval_jaxpr/ppermute | solution.py:15
  277.1 15.4 %collective-permute-start = (f32[12,128,128]{2,1,0:T(8,128)S(1)}, f32[12,128,128]{2,1,0:T(8,128)S(1)}, u32[]{:S(2)}, u32[]{:S(2)}) collective-permute-start(f32[12,128,128]{2,1,0:T(8,128)S(1)} %multiply_add_fusion.5), channel_id=1, source_target_pairs={{0,4},{4,8},{8,12},{12,16},{16,20},{20,24},{24,28},{28,32},{32,36}... | collective-permute-start | bytes 2359304 | tf_op jit(solution)/shard_map/while/body/eval_jaxpr/ppermute | solution.py:15
  293.3 15.4 %collective-permute-start = (f32[12,128,128]{2,1,0:T(8,128)S(1)}, f32[12,128,128]{2,1,0:T(8,128)S(1)}, u32[]{:S(2)}, u32[]{:S(2)}) collective-permute-start(f32[12,128,128]{2,1,0:T(8,128)S(1)} %multiply_add_fusion.5), channel_id=1, source_target_pairs={{0,4},{4,8},{8,12},{12,16},{16,20},{20,24},{24,28},{28,32},{32,36}... | collective-permute-start | bytes 2359304 | tf_op jit(solution)/shard_map/while/body/eval_jaxpr/ppermute | solution.py:15
  309.5 15.4 %collective-permute-start = (f32[12,128,128]{2,1,0:T(8,128)S(1)}, f32[12,128,128]{2,1,0:T(8,128)S(1)}, u32[]{:S(2)}, u32[]{:S(2)}) collective-permute-start(f32[12,128,128]{2,1,0:T(8,128)S(1)} %multiply_add_fusion.5), channel_id=1, source_target_pairs={{0,4},{4,8},{8,12},{12,16},{16,20},{20,24},{24,28},{28,32},{32,36}... | collective-permute-start | bytes 2359304 | tf_op jit(solution)/shard_map/while/body/eval_jaxpr/ppermute | solution.py:15
  325.8 15.4 %collective-permute-start = (f32[12,128,128]{2,1,0:T(8,128)S(1)}, f32[12,128,128]{2,1,0:T(8,128)S(1)}, u32[]{:S(2)}, u32[]{:S(2)}) collective-permute-start(f32[12,128,128]{2,1,0:T(8,128)S(1)} %multiply_add_fusion.5), channel_id=1, source_target_pairs={{0,4},{4,8},{8,12},{12,16},{16,20},{20,24},{24,28},{28,32},{32,36}... | collective-permute-start | bytes 2359304 | tf_op jit(solution)/shard_map/while/body/eval_jaxpr/ppermute | solution.py:15
  342.0 15.4 %collective-permute-start = (f32[12,128,128]{2,1,0:T(8,128)S(1)}, f32[12,128,128]{2,1,0:T(8,128)S(1)}, u32[]{:S(2)}, u32[]{:S(2)}) collective-permute-start(f32[12,128,128]{2,1,0:T(8,128)S(1)} %multiply_add_fusion.5), channel_id=1, source_target_pairs={{0,4},{4,8},{8,12},{12,16},{16,20},{20,24},{24,28},{28,32},{32,36}... | collective-permute-start | bytes 2359304 | tf_op jit(solution)/shard_map/while/body/eval_jaxpr/ppermute | solution.py:15
  358.2 15.4 %collective-permute-start = (f32[12,128,128]{2,1,0:T(8,128)S(1)}, f32[12,128,128]{2,1,0:T(8,128)S(1)}, u32[]{:S(2)}, u32[]{:S(2)}) collective-permute-start(f32[12,128,128]{2,1,0:T(8,128)S(1)} %multiply_add_fusion.5), channel_id=1, source_target_pairs={{0,4},{4,8},{8,12},{12,16},{16,20},{20,24},{24,28},{28,32},{32,36}... | collective-permute-start | bytes 2359304 | tf_op jit(solution)/shard_map/while/body/eval_jaxpr/ppermute | solution.py:15
  374.5 15.4 %collective-permute-start = (f32[12,128,128]{2,1,0:T(8,128)S(1)}, f32[12,128,128]{2,1,0:T(8,128)S(1)}, u32[]{:S(2)}, u32[]{:S(2)}) collective-permute-start(f32[12,128,128]{2,1,0:T(8,128)S(1)} %multiply_add_fusion.5), channel_id=1, source_target_pairs={{0,4},{4,8},{8,12},{12,16},{16,20},{20,24},{24,28},{28,32},{32,36}... | collective-permute-start | bytes 2359304 | tf_op jit(solution)/shard_map/while/body/eval_jaxpr/ppermute | solution.py:15
  390.7 15.4 %collective-permute-start = (f32[12,128,128]{2,1,0:T(8,128)S(1)}, f32[12,128,128]{2,1,0:T(8,128)S(1)}, u32[]{:S(2)}, u32[]{:S(2)}) collective-permute-start(f32[12,128,128]{2,1,0:T(8,128)S(1)} %multiply_add_fusion.5), channel_id=1, source_target_pairs={{0,4},{4,8},{8,12},{12,16},{16,20},{20,24},{24,28},{28,32},{32,36}... | collective-permute-start | bytes 2359304 | tf_op jit(solution)/shard_map/while/body/eval_jaxpr/ppermute | solution.py:15
  406.9 15.4 %collective-permute-start = (f32[12,128,128]{2,1,0:T(8,128)S(1)}, f32[12,128,128]{2,1,0:T(8,128)S(1)}, u32[]{:S(2)}, u32[]{:S(2)}) collective-permute-start(f32[12,128,128]{2,1,0:T(8,128)S(1)} %multiply_add_fusion.5), channel_id=1, source_target_pairs={{0,4},{4,8},{8,12},{12,16},{16,20},{20,24},{24,28},{28,32},{32,36}... | collective-permute-start | bytes 2359304 | tf_op jit(solution)/shard_map/while/body/eval_jaxpr/ppermute | solution.py:15
  423.1 15.4 %collective-permute-start = (f32[12,128,128]{2,1,0:T(8,128)S(1)}, f32[12,128,128]{2,1,0:T(8,128)S(1)}, u32[]{:S(2)}, u32[]{:S(2)}) collective-permute-start(f32[12,128,128]{2,1,0:T(8,128)S(1)} %multiply_add_fusion.5), channel_id=1, source_target_pairs={{0,4},{4,8},{8,12},{12,16},{16,20},{20,24},{24,28},{28,32},{32,36}... | collective-permute-start | bytes 2359304 | tf_op jit(solution)/shard_map/while/body/eval_jaxpr/ppermute | solution.py:15
  439.4 15.4 %collective-permute-start = (f32[12,128,128]{2,1,0:T(8,128)S(1)}, f32[12,128,128]{2,1,0:T(8,128)S(1)}, u32[]{:S(2)}, u32[]{:S(2)}) collective-permute-start(f32[12,128,128]{2,1,0:T(8,128)S(1)} %multiply_add_fusion.5), channel_id=1, source_target_pairs={{0,4},{4,8},{8,12},{12,16},{16,20},{20,24},{24,28},{28,32},{32,36}... | collective-permute-start | bytes 2359304 | tf_op jit(solution)/shard_map/while/body/eval_jaxpr/ppermute | solution.py:15
  455.6 15.4 %collective-permute-start = (f32[12,128,128]{2,1,0:T(8,128)S(1)}, f32[12,128,128]{2,1,0:T(8,128)S(1)}, u32[]{:S(2)}, u32[]{:S(2)}) collective-permute-start(f32[12,128,128]{2,1,0:T(8,128)S(1)} %multiply_add_fusion.5), channel_id=1, source_target_pairs={{0,4},{4,8},{8,12},{12,16},{16,20},{20,24},{24,28},{28,32},{32,36}... | collective-permute-start | bytes 2359304 | tf_op jit(solution)/shard_map/while/body/eval_jaxpr/ppermute | solution.py:15
  488.1 15.4 %collective-permute-start = (f32[12,128,128]{2,1,0:T(8,128)S(1)}, f32[12,128,128]{2,1,0:T(8,128)S(1)}, u32[]{:S(2)}, u32[]{:S(2)}) collective-permute-start(f32[12,128,128]{2,1,0:T(8,128)S(1)} %multiply_add_fusion.5), channel_id=1, source_target_pairs={{0,4},{4,8},{8,12},{12,16},{16,20},{20,24},{24,28},{28,32},{32,36}... | collective-permute-start | bytes 2359304 | tf_op jit(solution)/shard_map/while/body/eval_jaxpr/ppermute | solution.py:15
  504.3 15.4 %collective-permute-start = (f32[12,128,128]{2,1,0:T(8,128)S(1)}, f32[12,128,128]{2,1,0:T(8,128)S(1)}, u32[]{:S(2)}, u32[]{:S(2)}) collective-permute-start(f32[12,128,128]{2,1,0:T(8,128)S(1)} %multiply_add_fusion.5), channel_id=1, source_target_pairs={{0,4},{4,8},{8,12},{12,16},{16,20},{20,24},{24,28},{28,32},{32,36}... | collective-permute-start | bytes 2359304 | tf_op jit(solution)/shard_map/while/body/eval_jaxpr/ppermute | solution.py:15
  524.8 38.9 %all-to-all-start.1 = ((bf16[32,18,1536]{2,1,0:T(8,128)(2,1)}), bf16[32,18,1536]{2,1,0:T(8,128)(2,1)S(1)}, u32[]{:S(2)}, u32[]{:S(2)}) async-start(bf16[32,18,1536]{2,1,0:T(8,128)(2,1)} %bitcast.125), calls=%async_computation.1 | async-start | bytes 4718592 | tf_op jit(solution)/shard_map/all_to_all | solution.py:120
  566.6 38.0 %all-to-all-start = ((bf16[32,18,1536]{2,1,0:T(8,128)(2,1)}), bf16[32,18,1536]{2,1,0:T(8,128)(2,1)}, u32[]{:S(2)}, u32[]{:S(2)}) async-start(bf16[32,18,1536]{2,1,0:T(8,128)(2,1)} %bitcast.124), calls=%async_computation | async-start | bytes 4718592 | tf_op jit(solution)/shard_map/all_to_all | solution.py:121
  574.2 151.9 %all-reduce.3.cloned.1.call-start = ((), (), s32[]{:S(2)}) async-start(), calls=%async_computation.3 | async-start | bytes 10616832 | tf_op jit(solution)/shard_map/psum | solution.py:130
  (50 other events, 1578.8 us)
Sparse Core Ops, SparseCore 0:
  616.0 110.0 all-reduce.2
where the time goes:
time: 1310 us; the launch traced here: 1300 us
  waiting for transfers between devices  849 us (65%)
  starting transfers between devices  275 us (21%)
  other arithmetic  55.8 us (4%)
  matrix products  44.7 us (3%)
  blocking collectives  37.7 us (3%)
  local copies, waits for them, and re-layouts  24 us (2%)
  between operations  14.4 us (1%)
    ppermute x62, waiting for transfers between devices, from_behind(): return lax.ppermute(array, axis, pairs)  694 us
    ppermute x62, starting transfers between devices, from_behind(): return lax.ppermute(array, axis, pairs)  259 us
    psum x1, waiting for transfers between devices, on_device(): lax.psum(pre_part.astype(jnp.bfloat16), 'exp').astype(jnp.float32)  110 us
    all_to_all x1, blocking collectives, on_device(): lax.all_to_all(back_half, 'ctx', split_axis=0, concat_axis=0, tiled=True)  37.7 us
  transfers between devices with their start and end apart: 65, of which 65 were waited for; matrix products, arithmetic and copies ran while one was open for 1% of the time, Pallas kernels for 0%

commit v1 on v0

--- a/solution.py
+++ b/solution.py
@@ -1,18 +1,15 @@
+import functools
 import jax
 import jax.numpy as jnp
 from jax import lax
+from jax.experimental import pallas as pl
+from jax.experimental.pallas import tpu as pltpu
 from jax.sharding import PartitionSpec as P
 
 DH = 128
 
 
 HIGHEST = lax.Precision.HIGHEST
-
-
-def from_behind(array, axis, by):
-    peers = lax.axis_size(axis)
-    pairs = [(i, i + by) for i in range(peers) if 0 <= i + by < peers]
-    return lax.ppermute(array, axis, pairs)
 
 
 def silu_slope(value):
@@ -49,20 +46,88 @@
     return (jnp.sum(match, axis=2), jnp.sum(match * gate_block[None], axis=2))
 
 
-def forward_states(factor, local):
-
-    def forward_advance(step, incoming):
-        return from_behind(factor * incoming + local, "ctx", 1)
-
-    return lax.fori_loop(0, lax.axis_size("ctx") - 1, forward_advance, jnp.zeros_like(local))
-
-
-def reverse_states(factor, local):
-
-    def reverse_advance(step, incoming):
-        return from_behind(factor * incoming + local, "ctx", -1)
-
-    return lax.fori_loop(0, lax.axis_size("ctx") - 1, reverse_advance, jnp.zeros_like(local))
+MESH = pl.DeviceIdType.MESH
+
+
+def scan_kernel(reverse, rates_ref, local_ref, out_ref, got, made, send_a, recv_a, send_b, recv_b):
+    n = local_ref.shape[0]
+    rows = local_ref.shape[1]
+    me = lax.axis_index("ctx")
+    barrier = pltpu.get_barrier_semaphore()
+
+    def greet(k, carry):
+        pl.semaphore_signal(barrier, inc=1, device_id={"ctx": lax.rem(me + k, n)}, device_id_type=MESH)
+        return carry
+
+    lax.fori_loop(1, n, greet, 0)
+    got[me] = local_ref[me]
+    pl.semaphore_wait(barrier, n - 1)
+
+    def first(k):
+        peer = lax.rem(me + k, n)
+        return pltpu.make_async_remote_copy(
+            src_ref=local_ref.at[peer],
+            dst_ref=got.at[me],
+            send_sem=send_a.at[k],
+            recv_sem=recv_a.at[k],
+            device_id={"ctx": peer},
+            device_id_type=MESH,
+        )
+
+    def second(k):
+        peer = lax.rem(me + k, n)
+        return pltpu.make_async_remote_copy(
+            src_ref=made.at[peer],
+            dst_ref=out_ref.at[me],
+            send_sem=send_b.at[k],
+            recv_sem=recv_b.at[k],
+            device_id={"ctx": peer},
+            device_id_type=MESH,
+        )
+
+    def loop(action):
+        def body(k, carry):
+            action(k)
+            return carry
+
+        lax.fori_loop(1, n, body, 0)
+
+    loop(lambda k: first(k).start())
+    row = lax.broadcasted_iota(jnp.int32, (rows, DH), 0) + me * rows
+    rate = jnp.zeros((rows, DH), jnp.float32)
+    for head in range(rates_ref.shape[0]):
+        inside = (row >= head * DH) & (row < (head + 1) * DH)
+        rate = jnp.where(inside, rates_ref[head], rate)
+    factor = jnp.exp(-rate * float(DH))
+    loop(lambda k: first(k).wait_recv())
+
+    def step(i, total):
+        c = n - 1 - i if reverse else i
+        made[c] = total.astype(made.dtype)
+        return factor * total + got[c].astype(jnp.float32)
+
+    lax.fori_loop(0, n, step, jnp.zeros((rows, DH), jnp.float32))
+    loop(lambda k: second(k).start())
+    out_ref[me] = made[me]
+    loop(lambda k: second(k).wait_recv())
+    loop(lambda k: first(k).wait_send())
+    loop(lambda k: second(k).wait_send())
+
+
+def states(rates, local, reverse):
+    heads = local.shape[0]
+    n = lax.axis_size("ctx")
+    rows = heads * DH // n
+    pieces = local.astype(jnp.bfloat16).reshape(n, rows, DH)
+    out = pl.pallas_call(
+        functools.partial(scan_kernel, reverse),
+        out_shape=jax.ShapeDtypeStruct(pieces.shape, jnp.bfloat16),
+        in_specs=[pl.BlockSpec(memory_space=pltpu.SMEM), pl.BlockSpec(memory_space=pltpu.VMEM)],
+        out_specs=pl.BlockSpec(memory_space=pltpu.VMEM),
+        scratch_shapes=[pltpu.VMEM(pieces.shape, jnp.bfloat16)] * 2 + [pltpu.SemaphoreType.DMA((n,))] * 4,
+        compiler_params=pltpu.CompilerParams(collective_id=1 if reverse else 0, has_side_effects=True),
+    )(rates, pieces)
+    return out.reshape(heads, DH, DH).astype(jnp.float32)
 
 
 def contract_last(left, right):
@@ -79,7 +144,6 @@
     heads = group // DH
     scale = 1.0 / DH
     within, start_pow, end_pow, last_pow, next_pow, whole_pow = decay_tables(decay_rates, block_len)
-    factor = whole_pow[:, None, None]
     query_heads = queries.reshape(block_len, heads, DH)
     key_heads = keys.reshape(block_len, heads, DH)
     value_heads = values.reshape(block_len, heads, DH)
@@ -92,7 +156,7 @@
     key_local = jnp.einsum(
         "ihd,ihe->hde", key_wide * end_pow[:, :, None], value_wide, precision=HIGHEST
     )
-    entering = forward_states(factor, key_local)
+    entering = states(decay_rates, key_local, False)
     inter = (
         scale
         * start_pow[:, :, None]
@@ -149,7 +213,7 @@
     query_local = jnp.einsum(
         "ihd,ihe->hde", query_wide * next_pow[:, :, None], grad_wide, precision=HIGHEST
     )
-    leaving = reverse_states(factor, query_local)
+    leaving = states(decay_rates, query_local, True)
     dscores = jnp.einsum(
         "ihd,jhd->hij", grad_heads, value_heads, preferred_element_type=jnp.float32
     )

time: 1310 us -> 338 us (0.26)
  waiting for transfers between devices: 849 us -> 129 us
  starting transfers between devices: 275 us -> 15.4 us
  Pallas kernels: 0 us -> 58.8 us
  other arithmetic: 55.8 us -> 8.55 us
    ppermute x62 -> x0, waiting for transfers between devices: 694 us -> none  [from_behind(): return lax.ppermute(array, axis, pairs)]
    ppermute x62 -> x0, starting transfers between devices: 259 us -> none  [from_behind(): return lax.ppermute(array, axis, pairs)]
    pallas_call x0 -> x2, Pallas kernels: none -> 58.8 us  [states(): pl.pallas_call(functools.partial(scan_kernel, reverse), out_shape=jax.Sha...]
    add x62 -> x0, other arithmetic: 49.8 us -> none  [the longest x31 24.9 us: reverse_advance(): return from_behind(factor * incoming + local, 'ctx', -1)]
    all_to_all x1, waiting for transfers between devices: 19.2 us -> 0.01 us  [on_device(): lax.all_to_all(doubled(send_grad), 'ctx', split_axis=0, concat_axis=0, ti...]
  transfers between devices with their start and end apart: 65 -> 3, of which waited for: 65 -> 2; matrix products, arithmetic and copies ran while one was open for 1% -> 8% of each run, Pallas kernels for 0% -> 11%
where the time goes in v1:
time: 338 us; the launch traced here: 335 us
  waiting for transfers between devices  129 us (38%)
  Pallas kernels  58.8 us (17%)
  matrix products  48.8 us (14%)
  blocking collectives  37.7 us (11%)
  local copies, waits for them, and re-layouts  22 us (7%)
  starting transfers between devices  15.4 us (5%)
  between operations  14.4 us (4%)
  other arithmetic  8.55 us (3%)
    psum x1, waiting for transfers between devices, on_device(): lax.psum(pre_part.astype(jnp.bfloat16), 'exp').astype(jnp.float32)  110 us
    pallas_call x2, Pallas kernels, states(): pl.pallas_call(functools.partial(scan_kernel, reverse), out_shape=jax.Sha...  58.8 us
    all_to_all x1, blocking collectives, on_device(): lax.all_to_all(back_half, 'ctx', split_axis=0, concat_axis=0, tiled=True)  37.7 us
    dot_general x2, matrix products, contract_last(): lax.dot_general(left, right, (((1,), (1,)), ((), ())), preferred_element_...  20.3 us
    all_to_all x1, waiting for transfers between devices, on_device(): lax.all_to_all(doubled(send_in), 'ctx', split_axis=0, concat_axis=0, tile...  19.1 us
    all_to_all x1, starting transfers between devices, on_device(): lax.all_to_all(doubled(send_grad), 'ctx', split_axis=0, concat_axis=0, ti...  8.82 us
    dot_general x1, matrix products, on_device(): pre_part = jnp.dot(in_rows, up_local, preferred_element_type=jnp.float32)  8.53 us
    broadcast_in_dim x4, local copies, waits for them, and re-layouts, doubled(): jnp.broadcast_to(array.reshape(experts, 1, capacity, group), (experts, 2,...  7.09 us
  transfers between devices with their start and end apart: 3, of which 2 were waited for; matrix products, arithmetic and copies ran while one was open for 8% of the time, Pallas kernels for 11%

profile of v1, /device:TPU:7, one launch (start us, length us, event | category | flops | bytes accessed | tf_op | source)
XLA Modules:
  0.0 335.2 jit_solution(17914620066463050462)
XLA Ops:
  10.1 1.4 convert_reduce_fusion.1
  12.1 1.4 convolution_convert_fusion.1
  13.7 1.6 broadcast_in_dim.21
  15.4 8.8 %all-to-all-start = ((bf16[32,18,1536]{2,1,0:T(8,128)(2,1)}), bf16[32,18,1536]{2,1,0:T(8,128)(2,1)S(1)}, u32[]{:S(2)}, u32[]{:S(2)}) async-start(bf16[32,18,1536]{2,1,0:T(8,128)(2,1)} %bitcast.120), calls=%async_computation | async-start | bytes 4718592 | tf_op jit(solution)/shard_map/all_to_all | solution.py:185
  26.9 1.2 copy.93
  28.1 1.4 exponential_multiply_fusion
  29.5 1.7 convolution_convert_fusion.3
  31.1 38.0 %shard_map.112 = bf16[32,48,128]{2,1,0:T(8,128)(2,1)} custom-call(f32[12]{0:T(128)} %rates_ref.3, bf16[32,48,128]{2,1,0:T(8,128)(2,1)} %bitcast.142), custom_call_target="tpu_custom_call" | custom-call | tf_op jit(solution)/shard_map/pallas_call | solution.py:122
  70.8 1.0 fusion.36
  71.9 1.4 fusion.31
  73.8 1.3 convolution_convert_fusion
  75.1 2.3 broadcast_in_dim.24
  77.4 2.9 broadcast_in_dim.25
  80.3 6.4 %all-to-all-start.1 = ((bf16[32,18,1536]{2,1,0:T(8,128)(2,1)}), bf16[32,18,1536]{2,1,0:T(8,128)(2,1)}, u32[]{:S(2)}, u32[]{:S(2)}) async-start(bf16[32,18,1536]{2,1,0:T(8,128)(2,1)} %bitcast.121), calls=%async_computation.1 | async-start | bytes 4718592 | tf_op jit(solution)/shard_map/all_to_all | solution.py:184
  86.9 1.6 reshape.290
  88.5 9.4 %fusion.13 = bf16[576,2304]{1,0:T(8,128)(2,1)} fusion(bf16[576,1536]{1,0:T(8,128)(2,1)} %reshape.290, bf16[1,2304,1536]{2,1,0:T(8,128)(2,1)} %param.14), kind=kOutput, calls=%fused_computation.16 | convolution fusion | flops 4078190592 | bytes 11501568 | tf_op jit(solution)/shard_map/dot_general | solution.py:134
  97.9 19.1 %all-to-all-done.1 = bf16[32,18,1536]{2,1,0:T(8,128)(2,1)} async-done(((bf16[32,18,1536]{2,1,0:T(8,128)(2,1)}), bf16[32,18,1536]{2,1,0:T(8,128)(2,1)}, u32[]{:S(2)}, u32[]{:S(2)}) %all-to-all-start.1) | async-done | bytes 1769504 | tf_op jit(solution)/shard_map/all_to_all | solution.py:184
  117.0 2.6 reshape.298
  119.6 8.5 %fusion.16 = bf16[576,2304]{1,0:T(8,128)(2,1)} fusion(bf16[576,1536]{1,0:T(8,128)(2,1)S(1)} %reshape.298, bf16[1,1536,2304]{2,1,0:T(8,128)(2,1)} %param.13), kind=kOutput, calls=%fused_computation.17 | convolution fusion | flops 4078190592 | bytes 11501568 | tf_op jit(solution)/shard_map/dot_general | solution.py:191
  128.2 110.4 %all-reduce.3.cloned.1.call-done = (bf16[576,2304]{1,0:T(8,128)(2,1)}, bf16[576,2304]{1,0:T(8,128)(2,1)}) async-done(((bf16[576,2304]{1,0:T(8,128)(2,1)}, bf16[576,2304]{1,0:T(8,128)(2,1)}), (bf16[576,2304]{1,0:T(8,128)(2,1)}, bf16[576,2304]{1,0:T(8,128)(2,1)})) %all-reduce.3.cloned.1.call-update) | async-done | bytes 5308432 | tf_op jit(solution)/shard_map/psum | solution.py:194
  238.5 10.9 %fusion.19 = bf16[576,1536]{1,0:T(8,128)(2,1)} fusion(bf16[1,1536,2304]{2,1,0:T(8,128)(2,1)} %param.13, bf16[576,2304]{1,0:T(8,128)(2,1)} %get-tuple-element.17, bf16[576,2304]{1,0:T(8,128)(2,1)} %get-tuple-element.18), kind=kOutput, calls=%fused_computation.18 | convolution fusion | flops 4092346368 | bytes 14155776 | tf_op jit(solution)/shard_map/dot_general | solution.py:134
  249.5 2.5 reshape.299
  251.9 37.7 %all_to_all.15 = bf16[32,18,1536]{2,1,0:T(8,128)(2,1)S(1)} all-to-all(bf16[32,18,1536]{2,1,0:T(8,128)(2,1)S(1)} %reshape.299), channel_id=1, replica_groups=mesh['ctx'=32,'exp'=4] {'ctx'}, dimensions={0} | all-to-all | bytes 3538944 | tf_op jit(solution)/shard_map/all_to_all | solution.py:200
  290.1 1.5 reshape.302
  291.6 3.1 fusion.24
  295.0 1.1 fusion.35
  296.4 1.7 convolution_convert_fusion.2
  298.1 20.8 %shard_map.113 = bf16[32,48,128]{2,1,0:T(8,128)(2,1)} custom-call(f32[12]{0:T(128)} %rates_ref.3, bf16[32,48,128]{2,1,0:T(8,128)(2,1)} %bitcast.143), custom_call_target="tpu_custom_call" | custom-call | tf_op jit(solution)/shard_map/pallas_call | solution.py:122
  318.9 2.3 fusion.26
  321.2 1.3 fusion.28
  322.5 1.4 fusion.38
  324.8 1.4 fusion.39
  (62 shorter events, 12.7 us)
Async XLA Ops:
  11.5 0.6 copy-start.4
  15.4 10.5 %copy-start.13 = (f32[12]{0:T(128)S(1)}, f32[12]{0:T(128)}, u32[]{:S(2)}) copy-start(f32[12]{0:T(128)} %rates_ref.3) | copy-start | bytes 148
  15.4 11.0 %copy-start.6 = (bf16[128,1536]{1,0:T(8,128)(2,1)S(1)}, bf16[128,1536]{1,0:T(8,128)(2,1)}, u32[]{:S(2)}) copy-start(bf16[128,1536]{1,0:T(8,128)(2,1)} %param.9) | copy-start | bytes 1179652
  15.4 11.3 %copy-start.7 = (bf16[128,1536]{1,0:T(8,128)(2,1)S(1)}, bf16[128,1536]{1,0:T(8,128)(2,1)}, u32[]{:S(2)}) copy-start(bf16[128,1536]{1,0:T(8,128)(2,1)} %param.10) | copy-start | bytes 1179652
  15.4 62.0 %all-to-all-start = ((bf16[32,18,1536]{2,1,0:T(8,128)(2,1)}), bf16[32,18,1536]{2,1,0:T(8,128)(2,1)S(1)}, u32[]{:S(2)}, u32[]{:S(2)}) async-start(bf16[32,18,1536]{2,1,0:T(8,128)(2,1)} %bitcast.120), calls=%async_computation | async-start | bytes 4718592 | tf_op jit(solution)/shard_map/all_to_all | solution.py:185
  70.0 1.9 copy-start.11
  70.8 1.1 copy-start.8
  70.8 2.9 copy-start.5
  71.9 1.9 copy-start.1
  80.3 36.7 %all-to-all-start.1 = ((bf16[32,18,1536]{2,1,0:T(8,128)(2,1)}), bf16[32,18,1536]{2,1,0:T(8,128)(2,1)}, u32[]{:S(2)}, u32[]{:S(2)}) async-start(bf16[32,18,1536]{2,1,0:T(8,128)(2,1)} %bitcast.121), calls=%async_computation.1 | async-start | bytes 4718592 | tf_op jit(solution)/shard_map/all_to_all | solution.py:184
  86.7 151.8 %all-reduce.3.cloned.1.call-start = ((), (), s32[]{:S(2)}) async-start(), calls=%async_computation.3 | async-start | bytes 10616832 | tf_op jit(solution)/shard_map/psum | solution.py:194
  291.6 3.4 %copy-start.9 = (f32[128,128]{1,0:T(8,128)S(1)}, f32[128,128]{1,0:T(8,128)}, u32[]{:S(2)}) copy-start(f32[128,128]{1,0:T(8,128)} %copy-done.8) | copy-start | bytes 196612
  291.6 3.4 %copy-start.12 = (pred[128,128]{1,0:T(8,128)(4,1)S(1)}, pred[128,128]{1,0:T(8,128)(4,1)}, u32[]{:S(2)}) copy-start(pred[128,128]{1,0:T(8,128)(4,1)} %copy-done.11) | copy-start | bytes 49156
  291.6 3.4 %copy-start.14 = (f32[12]{0:T(128)S(1)}, f32[12]{0:T(128)}, u32[]{:S(2)}) copy-start(f32[12]{0:T(128)} %neg.12) | copy-start | bytes 148
  291.6 4.5 %copy-start = (bf16[32,48,128]{2,1,0:T(8,128)(2,1)S(1)}, bf16[32,48,128]{2,1,0:T(8,128)(2,1)}, u32[]{:S(2)}) copy-start(bf16[32,48,128]{2,1,0:T(8,128)(2,1)} %shard_map.112) | copy-start | bytes 1179652
  294.7 1.7 copy-start.10
  318.9 5.9 %copy-start.2 = (bf16[12,128,128]{2,1,0:T(8,128)(2,1)S(1)}, bf16[12,128,128]{2,1,0:T(8,128)(2,1)}, u32[]{:S(2)}) copy-start(bf16[12,128,128]{2,1,0:T(8,128)(2,1)} %copy-done.1) | copy-start | bytes 1179652
  323.9 2.3 copy-start.3
Sparse Core Ops, SparseCore 0:
  128.3 110.2 all-reduce.2

commit v2 on v0

v2 whole, which is shorter than its diff:
```python
import jax
import jax.numpy as jnp
from jax import lax
from jax.experimental import pallas as pl
from jax.experimental.pallas import tpu as pltpu
from jax.sharding import PartitionSpec as P

DH = 128
MESH = pl.DeviceIdType.MESH
BF = jnp.bfloat16
F32 = jnp.float32
CHUNKS = (8, 8)
MAIN = 16
EXTRA = 2
QUARTERS = 4


def nn(left, right):
    return lax.dot_general(left, right, (((1,), (0,)), ((), ())), preferred_element_type=F32)


def nt(left, right):
    return lax.dot_general(left, right, (((1,), (1,)), ((), ())), preferred_element_type=F32)


def tn(left, right):
    return lax.dot_general(left, right, (((0,), (0,)), ((), ())), preferred_element_type=F32)


def iota(shape, dim):
    return lax.broadcasted_iota(jnp.int32, shape, dim)


def each(lower, upper, action):
    def body(i, carry):
        action(i)
        return carry

    lax.fori_loop(lower, upper, body, 0)


class Remote:
    def __init__(self, make):
        self.make = make

    def start(self, *index):
        self.make(*index).start()

    def arrived(self, *index):
        self.make(*index).wait_recv()

    def left(self, *index):
        self.make(*index).wait_send()


def layer_kernel(
    rates, routes, gates, queries, keys, values, out_grad, up_hbm, down_hbm,
    query_g, key_g, value_g,
    up, down, main_hot, extra_hot, send_main, send_extra, rows_in, extra_in, partial,
    turned, below, above, slope, back, crossed, final, home_extra_out, home, home_extra,
    weights, intra, attn, local, got, made, entering, local_b, got_b, made_b, leaving, grad_out,
    key_part, value_part,
    weight_sem, main_s, main_r, relay_s, relay_r, extra_s, extra_r, hop_s, hop_r,
    fore_s, fore_r, rear_s, rear_r, reduce_s, reduce_r, gather_s, gather_r, cross_s, cross_r,
    home_s, home_r, homex_s, homex_r,
):
    block = queries.shape[0]
    group = queries.shape[1]
    heads = group // DH
    hidden = up.shape[1]
    half = hidden // 2
    quarter = group // QUARTERS
    scale = 1.0 / DH
    ctx = lax.axis_size("ctx")
    chips = ctx // 2
    me = lax.axis_index("ctx")
    level = lax.axis_index("exp")
    chip = lax.div(me, 2)
    core = lax.rem(me, 2)
    partner = me + 1 - 2 * core
    nxt, opp, prv = (lax.rem(level + i, 4) for i in (1, 2, 3))

    barrier = pltpu.get_barrier_semaphore()
    each(1, ctx, lambda k: pl.semaphore_signal(
        barrier, inc=1, device_id={"ctx": lax.rem(me + k, ctx)}, device_id_type=MESH))
    for peer in (nxt, prv):
        pl.semaphore_signal(barrier, inc=1, device_id={"exp": peer}, device_id_type=MESH)
    load_down = pltpu.make_async_copy(down_hbm.at[0], down, weight_sem.at[0])
    load_up = pltpu.make_async_copy(up_hbm.at[0], up, weight_sem.at[1])
    load_down.start()
    load_up.start()

    spans, base, short, first = [], 0, 0, 0
    for number, n in enumerate(CHUNKS):
        tall = 8 * n + (MAIN if number == 0 else 0)
        spans.append((first, n, base, tall, short))
        first, base, short = first + n, base + 4 * tall, short + tall

    def block_row(number, owner_base, local_k):
        first_k, n, start, tall, _ = spans[number]
        each_owner = n // 2
        owner = owner_base + lax.div(local_k, each_owner)
        return pl.multiple_of(start + owner * tall + lax.rem(local_k, each_owner) * MAIN, MAIN)

    expert = iota((block, chips), 1)
    hits = [(routes[:, k : k + 1] == expert).astype(F32) for k in range(2)]
    earlier = (iota((block, block), 1) < iota((block, block), 0)).astype(BF)
    before = nn(earlier, (hits[0] + hits[1]).astype(BF))
    for k in range(2):
        placed = jnp.sum(before * hits[k], axis=1, keepdims=True).astype(jnp.int32)
        chosen = routes[:, k : k + 1]
        target = jnp.where(placed < MAIN, chosen * MAIN + placed, -1)
        main_hot[k] = (target == iota((block, chips * MAIN), 1)).astype(F32).astype(BF)
        spare = jnp.where(placed >= MAIN, chosen * 8 + placed - MAIN, -64)
        for q in range(QUARTERS):
            extra_hot[k, q] = (spare + EXTRA * q == iota((block, chips * 8), 1)).astype(F32).astype(BF)

    def gather(a, source):
        pick = main_hot[0] + main_hot[1]

        def columns(i):
            cols = pl.ds(pl.multiple_of(i * 256, 256), 256)
            send_main[a, :, cols] = tn(pick, source[:, cols]).astype(BF)

        each(0, group // 256, columns)
        total = jnp.zeros((chips * 8, quarter), F32)
        for q in range(QUARTERS):
            total += tn(extra_hot[0, q] + extra_hot[1, q], source[:, q * quarter : (q + 1) * quarter])
        send_extra[a] = total.astype(BF).reshape(chips, 8, quarter)

    def same_core(k):
        return lax.rem(chip + k, chips) * 2 + core

    def dispatch(a, number):
        first_k = spans[number][0]

        def make(k):
            return pltpu.make_async_remote_copy(
                src_ref=send_main.at[a, pl.ds(pl.multiple_of(lax.rem(chip + k, chips) * MAIN, MAIN), MAIN), :],
                dst_ref=rows_in.at[a, pl.ds(block_row(number, 2 * core, k - first_k), MAIN), :],
                send_sem=main_s.at[a, k], recv_sem=main_r.at[a, k],
                device_id={"ctx": same_core(k)}, device_id_type=MESH)

        return Remote(make)

    def relay(a, number, side):
        first_k = spans[number][0]

        def make(k):
            rows = rows_in.at[a, pl.ds(block_row(number, 2 * side, k - first_k), MAIN), :]
            return pltpu.make_async_remote_copy(
                src_ref=rows, dst_ref=rows, send_sem=relay_s.at[a, k], recv_sem=relay_r.at[a, k],
                device_id={"ctx": partner}, device_id_type=MESH)

        return Remote(make)

    def dispatch_extra(a):
        def make(k):
            return pltpu.make_async_remote_copy(
                src_ref=send_extra.at[a, lax.rem(chip + k, chips)], dst_ref=extra_in.at[a, core * chips + k],
                send_sem=extra_s.at[a, k], recv_sem=extra_r.at[a, k],
                device_id={"ctx": same_core(k)}, device_id_type=MESH)

        return Remote(make)

    def relay_extra(a, side):
        def make(k):
            rows = extra_in.at[a, side * chips + k]
            return pltpu.make_async_remote_copy(
                src_ref=rows, dst_ref=rows, send_sem=hop_s.at[a, k], recv_sem=hop_r.at[a, k],
                device_id={"ctx": partner}, device_id_type=MESH)

        return Remote(make)

    def send_rows(a, number):
        first_k, n = spans[number][:2]
        if number == 0:
            extra = dispatch_extra(a)
            each(1, chips, extra.start)
            extra_in[a, core * chips] = send_extra[a, chip]
            relay_extra(a, core).start(0)
            mine = send_main[a, pl.ds(pl.multiple_of(chip * MAIN, MAIN), MAIN), :]
            rows_in[a, pl.ds(block_row(0, 2 * core, 0), MAIN), :] = mine
            relay(a, 0, core).start(0)
        each(max(first_k, 1), first_k + n, dispatch(a, number).start)

    def pass_on(a, number):
        first_k, n = spans[number][:2]
        if number == 0:
            arriving, onward = dispatch_extra(a), relay_extra(a, core)

            def step(k):
                arriving.arrived(k)
                onward.start(k)

            each(1, chips, step)
        arriving_rows, onward_rows = dispatch(a, number), relay(a, number, core)

        def row_step(k):
            arriving_rows.arrived(k)
            onward_rows.start(k)

        each(max(first_k, 1), first_k + n, row_step)

    def all_rows(a, number):
        first_k, n, start, tall, _ = spans[number]
        if number == 0:
            each(0, chips, relay_extra(a, 1 - core).arrived)
        each(first_k, first_k + n, relay(a, number, 1 - core).arrived)
        if number == 0:
            packed = extra_in[a].reshape(2 * chips * 8, quarter)
            count = 2 * chips * EXTRA
            row, col = iota((count, 2 * chips * 8), 0), iota((count, 2 * chips * 8), 1)
            origin = lax.div(row, 2) * 8 + lax.rem(row, 2)
            for q in range(QUARTERS):
                placed = nn((col == origin + EXTRA * q).astype(F32).astype(BF), packed).astype(BF)
                for owner in range(4):
                    at = start + owner * tall + tall - MAIN
                    rows_in[a, at : at + MAIN, q * quarter : (q + 1) * quarter] = placed[owner * MAIN : (owner + 1) * MAIN]

    def expert_in(a, number):
        start, tall = spans[number][2:4]

        def columns(i):
            at = pl.multiple_of(i * 256, 256)
            rows = rows_in[a, start : start + 4 * tall, :]
            if a == 0:
                product = nt(rows, down[pl.ds(at, 256), :])
            else:
                product = nn(rows, up[:, pl.ds(at, 256)])
            partial[a, start : start + 4 * tall, pl.ds(at, 256)] = product.astype(BF)

        each(0, hidden // 256, columns)

    low, high = pl.ds(0, half), pl.ds(half, half)

    def reducer(a, number, which):
        _, _, start, tall, rest = spans[number]

        def owned(by):
            return pl.ds(pl.multiple_of(start + by * tall, MAIN), tall)

        there = pl.ds(rest, tall)
        src, dst, peer = {
            "turn_up": ((owned(opp), low), (turned, 0, low), nxt),
            "turn_down": ((owned(opp), high), (turned, 0, high), prv),
            "own_up": ((owned(nxt), high), (below, 0, high), nxt),
            "own_down": ((owned(prv), low), (above, 0, low), prv),
            "sum_up": ((owned(nxt), low), (below, 0, low), nxt),
            "sum_down": ((owned(prv), high), (above, 0, high), prv),
        }[which]
        slot = ("turn_up", "turn_down", "own_up", "own_down", "sum_up", "sum_down").index(which)
        return pltpu.make_async_remote_copy(
            src_ref=partial.at[a, src[0], src[1]], dst_ref=dst[0].at[a, there, dst[2]],
            send_sem=reduce_s.at[a, number, slot], recv_sem=reduce_r.at[a, number, slot],
            device_id={"exp": peer}, device_id_type=MESH)

    def reduce_start(a, number):
        for which in ("turn_up", "turn_down", "own_up", "own_down"):
            reducer(a, number, which).start()

    def reduce_turn(a, number):
        _, _, start, tall, rest = spans[number]
        wide = half // 3
        for turn, onward, by, offset in (("turn_up", "sum_up", nxt, 0), ("turn_down", "sum_down", prv, half)):
            reducer(a, number, turn).wait_recv()
            rows = pl.ds(pl.multiple_of(start + by * tall, MAIN), tall)

            def columns(i):
                cols = pl.ds(pl.multiple_of(offset + i * wide, 128), wide)
                mine = partial[a, rows, cols].astype(F32) + turned[a, rest : rest + tall, cols].astype(F32)
                partial[a, rows, cols] = mine.astype(BF)

            each(0, 3, columns)
            reducer(a, number, onward).start()

    def finish(number):
        _, _, start, tall, rest = spans[number]
        for a in range(2):
            for which in ("own_up", "own_down", "sum_up", "sum_down"):
                reducer(a, number, which).wait_recv()
        rows = pl.ds(pl.multiple_of(start + level * tall, MAIN), tall)
        there = pl.ds(rest, tall)

        def columns(i):
            cols = pl.ds(pl.multiple_of(i * 128, 128), 128)

            def total(a):
                return (partial[a, rows, cols].astype(F32) + below[a, there, cols].astype(F32)
                        + above[a, there, cols].astype(F32))

            pre = total(1)
            sigma = jax.nn.sigmoid(pre)
            slope[rows, cols] = (total(0) * (sigma * (1.0 + pre * (1.0 - sigma)))).astype(BF)

        each(0, hidden // 128, columns)
        for which in ("up_low", "down_high", "up_high", "down_low"):
            spread(number, which).start()

    def spread(number, which):
        _, _, start, tall, _ = spans[number]

        def owned(by):
            return pl.ds(pl.multiple_of(start + by * tall, MAIN), tall)

        owner, cols, peer = {
            "up_low": (level, low, nxt),
            "up_high": (level, high, nxt),
            "down_high": (level, high, prv),
            "down_low": (level, low, prv),
            "on_up": (prv, low, nxt),
            "on_down": (nxt, high, prv),
        }[which]
        slot = ("up_low", "up_high", "down_high", "down_low", "on_up", "on_down").index(which)
        rows = slope.at[owned(owner), cols]
        return pltpu.make_async_remote_copy(
            src_ref=rows, dst_ref=rows,
            send_sem=gather_s.at[number, slot], recv_sem=gather_r.at[number, slot],
            device_id={"exp": peer}, device_id_type=MESH)

    def spread_on(number):
        spread(number, "up_low").wait_recv()
        spread(number, "on_up").start()
        spread(number, "down_high").wait_recv()
        spread(number, "on_down").start()

    def spread_done(number):
        for which in ("up_high", "down_low", "on_up", "on_down"):
            spread(number, which).wait_recv()

    def cross(number, side, piece):
        _, _, start, tall, rest = spans[number]
        cols = pl.ds(piece * (group // 2), group // 2)
        return pltpu.make_async_remote_copy(
            src_ref=back.at[pl.ds(pl.multiple_of(start + side * 2 * tall, MAIN), 2 * tall), cols],
            dst_ref=crossed.at[pl.ds(2 * rest, 2 * tall), cols],
            send_sem=cross_s.at[number, piece], recv_sem=cross_r.at[number, piece],
            device_id={"ctx": partner}, device_id_type=MESH)

    def expert_back(number):
        _, _, start, tall, _ = spans[number]

        def columns(i):
            at = pl.multiple_of(i * 256, 256)
            product = nt(slope[start : start + 4 * tall, :], up[pl.ds(at, 256), :])
            back[start : start + 4 * tall, pl.ds(at, 256)] = product.astype(BF)

        for piece in range(2):
            each(piece * 3, piece * 3 + 3, columns)
            cross(number, 1 - core, piece).start()

    def go_home(number):
        first_k, n, start, tall, rest = spans[number]

        def make(k):
            local_k = k - first_k
            row = 2 * rest + lax.div(local_k, n // 2) * tall + lax.rem(local_k, n // 2) * MAIN
            return pltpu.make_async_remote_copy(
                src_ref=final.at[pl.ds(pl.multiple_of(row, MAIN), MAIN), :],
                dst_ref=home.at[pl.ds(pl.multiple_of(chip * MAIN, MAIN), MAIN), :],
                send_sem=home_s.at[k], recv_sem=home_r.at[k],
                device_id={"ctx": same_core(chips - k)}, device_id_type=MESH)

        return Remote(make)

    def extra_home():
        def make(k):
            return pltpu.make_async_remote_copy(
                src_ref=home_extra_out.at[k], dst_ref=home_extra.at[chip],
                send_sem=homex_s.at[k], recv_sem=homex_r.at[k],
                device_id={"ctx": same_core(chips - k)}, device_id_type=MESH)

        return Remote(make)

    def return_rows(number):
        first_k, n, start, tall, rest = spans[number]
        own = pl.multiple_of(start + core * 2 * tall, MAIN)
        for piece in range(2):
            cross(number, core, piece).wait_recv()

            def columns(i):
                cols = pl.ds(pl.multiple_of(i * 256, 256), 256)
                mine = back[pl.ds(own, 2 * tall), cols].astype(F32)
                mine += crossed[2 * rest : 2 * rest + 2 * tall, cols].astype(F32)
                final[2 * rest : 2 * rest + 2 * tall, cols] = mine.astype(BF)

            each(piece * 3, piece * 3 + 3, columns)
        if number == 0:
            count = chips * EXTRA
            row, col = iota((chips * 8, count), 1), iota((chips * 8, count), 0)
            origin = lax.div(row, 2) * 8 + lax.rem(row, 2)
            total = jnp.zeros((chips * 8, quarter), F32)
            for q in range(QUARTERS):
                cols = slice(q * quarter, (q + 1) * quarter)
                spare = jnp.concatenate(
                    [final[2 * rest + (o + 1) * tall - MAIN : 2 * rest + (o + 1) * tall, cols] for o in range(2)], axis=0)
                total += nn((col == origin + EXTRA * q).astype(F32).astype(BF), spare)
            home_extra_out[...] = total.astype(BF).reshape(chips, 8, quarter)
            each(1, chips, extra_home().start)
            home_extra[chip] = home_extra_out[0]
            home[pl.ds(pl.multiple_of(chip * MAIN, MAIN), MAIN), :] = final[2 * rest : 2 * rest + MAIN, :]
        each(max(first_k, 1), first_k + n, go_home(number).start)

    pieces = local.shape[0] // ctx

    def piece_rows(number):
        return pl.ds(pl.multiple_of(number * pieces, MAIN), pieces)

    def scan_out(source, target, sems):
        def make(k):
            peer = lax.rem(me + k, ctx)
            return pltpu.make_async_remote_copy(
                src_ref=source.at[piece_rows(peer), :], dst_ref=target.at[piece_rows(me), :],
                send_sem=sems[0].at[sems[2], k], recv_sem=sems[1].at[sems[2], k],
                device_id={"ctx": peer}, device_id_type=MESH)

        return Remote(make)

    def scan_local(arrived, prefixes, reverse):
        row = iota((pieces, DH), 0) + me * pieces
        rate = jnp.zeros((pieces, DH), F32)
        for h in range(heads):
            rate = jnp.where((row >= h * DH) & (row < (h + 1) * DH), rates[h], rate)
        factor = jnp.exp(-rate * float(block))

        def step(i, total):
            at = piece_rows(ctx - 1 - i if reverse else i)
            prefixes[at, :] = total.astype(BF)
            return factor * total + arrived[at, :].astype(F32)

        lax.fori_loop(0, ctx, step, jnp.zeros((pieces, DH), F32))

    fore, fore_back = (local, got, (fore_s, fore_r, 0)), (made, entering, (fore_s, fore_r, 1))
    rear, rear_back = (local_b, got_b, (rear_s, rear_r, 0)), (made_b, leaving, (rear_s, rear_r, 1))
    place = iota((block, DH), 0).astype(F32)

    def head_cols(h):
        return slice(h * DH, (h + 1) * DH)

    def scan_first(path):
        each(1, ctx, scan_out(*path).start)
        path[1][piece_rows(me), :] = path[0][piece_rows(me), :]

    def scan_second(path, path_back, reverse):
        each(1, ctx, scan_out(*path).arrived)
        scan_local(path[1], path_back[0], reverse)
        each(1, ctx, scan_out(*path_back).start)
        path_back[1][piece_rows(me), :] = path_back[0][piece_rows(me), :]

    def within(h):
        distance = (iota((block, block), 0) - iota((block, block), 1)).astype(F32)
        return jnp.where(distance >= 0.0, jnp.exp(-rates[h] * jnp.maximum(distance, 0.0)), 0.0)

    gather(0, out_grad)
    pl.semaphore_wait(barrier, ctx - 1 + 2)
    send_rows(0, 0)
    for h in range(heads):
        faded = (keys[:, head_cols(h)].astype(F32) * jnp.exp(-rates[h] * (float(block) - place))).astype(BF)
        local[h * DH : (h + 1) * DH, :] = tn(faded, values[:, head_cols(h)]).astype(BF)
    scan_first(fore)
    for number in range(1, len(CHUNKS)):
        send_rows(0, number)
    for h in range(heads):
        score = nt(queries[:, head_cols(h)], keys[:, head_cols(h)])
        weight = (scale * score * within(h)).astype(BF)
        weights[h] = weight
        intra[:, head_cols(h)] = nn(weight, values[:, head_cols(h)])
    pass_on(0, 0)
    scan_second(fore, fore_back, False)
    all_rows(0, 0)
    load_down.wait()
    expert_in(0, 0)
    reduce_start(0, 0)
    for number in range(1, len(CHUNKS)):
        pass_on(0, number)
    each(1, ctx, scan_out(*fore_back).arrived)
    for h in range(heads):
        across = nn(queries[:, head_cols(h)], entering[h * DH : (h + 1) * DH, :])
        total = intra[:, head_cols(h)] + scale * jnp.exp(-rates[h] * place) * across
        attn[:, head_cols(h)] = total.astype(BF)
    gather(1, attn)
    for number in range(len(CHUNKS)):
        send_rows(1, number)
    for number in range(1, len(CHUNKS)):
        all_rows(0, number)
        expert_in(0, number)
        reduce_start(0, number)
        reduce_turn(0, number - 1)
    pass_on(1, 0)
    reduce_turn(0, len(CHUNKS) - 1)
    all_rows(1, 0)
    load_up.wait()
    expert_in(1, 0)
    reduce_start(1, 0)
    for number in range(1, len(CHUNKS)):
        pass_on(1, number)
        reduce_turn(1, number - 1)
        all_rows(1, number)
        expert_in(1, number)
        reduce_start(1, number)
        finish(number - 1)
        reduce_turn(1, number)
        spread_on(number - 1)
    finish(len(CHUNKS) - 1)
    for number in range(len(CHUNKS)):
        spread_done(number)
        expert_back(number)
        if number + 1 < len(CHUNKS):
            spread_on(number + 1)
        return_rows(number)

    each(1, chips, extra_home().arrived)
    for number, (first_k, n, *_) in enumerate(spans):
        each(max(first_k, 1), first_k + n, go_home(number).arrived)
    for q in range(QUARTERS):
        cols = slice(q * quarter, (q + 1) * quarter)
        total = out_grad[:, cols].astype(F32)
        for k in range(2):
            mine = nn(main_hot[k], home[:, cols])
            mine += nn(extra_hot[k, q], home_extra[...].reshape(chips * 8, quarter))
            total += gates[:, k : k + 1] * mine
        grad_out[:, cols] = total.astype(BF)
    for h in range(heads):
        faded = (queries[:, head_cols(h)].astype(F32) * jnp.exp(-rates[h] * (place + 1.0))).astype(BF)
        local_b[h * DH : (h + 1) * DH, :] = tn(faded, grad_out[:, head_cols(h)]).astype(BF)
    scan_first(rear)
    for h in range(heads):
        cols = head_cols(h)
        grad = grad_out[:, cols]
        dweight = (scale * nt(grad, values[:, cols]) * within(h)).astype(BF)
        across = nt(grad, entering[h * DH : (h + 1) * DH, :])
        query_g[:, cols] = (nn(dweight, keys[:, cols]) + scale * jnp.exp(-rates[h] * place) * across).astype(BF)
        key_part[:, cols] = tn(dweight, queries[:, cols])
        value_part[:, cols] = tn(weights[h], grad)
    scan_second(rear, rear_back, True)
    each(1, ctx, scan_out(*rear_back).arrived)
    for h in range(heads):
        cols = head_cols(h)
        state = leaving[h * DH : (h + 1) * DH, :]
        fade = scale * jnp.exp(-rates[h] * (float(block) - 1.0 - place))
        key_g[:, cols] = (key_part[:, cols] + fade * nt(values[:, cols], state)).astype(BF)
        value_g[:, cols] = (value_part[:, cols] + fade * nn(keys[:, cols], state)).astype(BF)

    for path in (fore, fore_back, rear, rear_back):
        each(1, ctx, scan_out(*path).left)
    for a in range(2):
        each(1, chips, dispatch_extra(a).left)
        each(0, chips, relay_extra(a, core).left)
        for number, (first_k, n, *_) in enumerate(spans):
            each(max(first_k, 1), first_k + n, dispatch(a, number).left)
            each(first_k, first_k + n, relay(a, number, core).left)
            for which in ("turn_up", "turn_down", "own_up", "own_down", "sum_up", "sum_down"):
                reducer(a, number, which).wait_send()
    each(1, chips, extra_home().left)
    for number, (first_k, n, *_) in enumerate(spans):
        each(max(first_k, 1), first_k + n, go_home(number).left)
        for piece in range(2):
            cross(number, 1 - core, piece).wait_send()
        for which in ("up_low", "up_high", "down_high", "down_low", "on_up", "on_down"):
            spread(number, which).wait_send()


def on_device(
    queries, keys, values, out_grad, up_weight, down_weight, decay_rates, routes, gate_weights
):
    block, group = queries.shape
    heads = group // DH
    hidden = up_weight.shape[2]
    ctx = lax.axis_size("ctx")
    chips = ctx // 2
    slots = chips * MAIN
    total = 2 * chips * (MAIN + EXTRA)
    quarter = group // QUARTERS
    count = len(CHUNKS)
    state = (heads * DH, DH)
    dma = pltpu.SemaphoreType.DMA
    whole = pl.BlockSpec(memory_space=pltpu.VMEM)
    raw = pl.BlockSpec(memory_space=pl.ANY)
    out = jax.ShapeDtypeStruct((block, group), BF)
    return pl.pallas_call(
        layer_kernel,
        out_shape=(out, out, out),
        in_specs=[pl.BlockSpec(memory_space=pltpu.SMEM)] + [whole] * 6 + [raw] * 2,
        out_specs=(whole, whole, whole),
        scratch_shapes=[
            pltpu.VMEM((group, hidden), BF),
            pltpu.VMEM((hidden, group), BF),
            pltpu.VMEM((2, block, slots), BF),
            pltpu.VMEM((2, QUARTERS, block, chips * 8), BF),
            pltpu.VMEM((2, slots, group), BF),
            pltpu.VMEM((2, chips, 8, quarter), BF),
            pltpu.VMEM((2, total, group), BF),
            pltpu.VMEM((2, 2 * chips, 8, quarter), BF),
            pltpu.VMEM((2, total, hidden), BF),
            pltpu.VMEM((2, total // 4, hidden), BF),
            pltpu.VMEM((2, total // 4, hidden), BF),
            pltpu.VMEM((2, total // 4, hidden), BF),
            pltpu.VMEM((total, hidden), BF),
            pltpu.VMEM((total, group), BF),
            pltpu.VMEM((total // 2, group), BF),
            pltpu.VMEM((total // 2, group), BF),
            pltpu.VMEM((chips, 8, quarter), BF),
            pltpu.VMEM((slots, group), BF),
            pltpu.VMEM((chips, 8, quarter), BF),
            pltpu.VMEM((heads, block, block), BF),
            pltpu.VMEM((block, group), F32),
            pltpu.VMEM((block, group), BF),
        ]
        + [pltpu.VMEM(state, BF)] * 8
        + [
            pltpu.VMEM((block, group), BF),
            pltpu.VMEM((block, group), F32),
            pltpu.VMEM((block, group), F32),
            dma((2,)),
        ]
        + [dma((2, chips))] * 8
        + [dma((2, ctx))] * 4
        + [dma((2, count, 6))] * 2
        + [dma((count, 6))] * 2
        + [dma((count, 2))] * 2
        + [dma((chips,))] * 4,
        compiler_params=pltpu.CompilerParams(
            collective_id=0, has_side_effects=True, vmem_limit_bytes=67043328
        ),
    )(decay_rates, routes, gate_weights, queries, keys, values, out_grad, up_weight, down_weight)


def solution(mesh):
    placed = (
        P("ctx", "exp"),
        P("ctx", "exp"),
        P("ctx", "exp"),
        P("ctx", "exp"),
        P("ctx", "exp", None),
        P("ctx", None, "exp"),
        P("exp"),
        P("ctx", None),
        P("ctx", None),
    )
    return jax.shard_map(
        on_device,
        mesh=mesh,
        in_specs=placed,
        out_specs=(P("ctx", "exp"), P("ctx", "exp"), P("ctx", "exp")),
        check_vma=False,
    )
```

time: 1310 us -> 146 us (0.11)
  waiting for transfers between devices: 849 us -> 0 us
  starting transfers between devices: 275 us -> 0 us
  Pallas kernels: 0 us -> 135 us
  other arithmetic: 55.8 us -> 0 us
  matrix products: 44.7 us -> 0 us
  blocking collectives: 37.7 us -> 0 us
  local copies, waits for them, and re-layouts: 24 us -> 8.13 us
  between operations: 14.4 us -> 0.64 us
    ppermute x62 -> x0, waiting for transfers between devices: 694 us -> none  [from_behind(): return lax.ppermute(array, axis, pairs)]
    ppermute x62 -> x0, starting transfers between devices: 259 us -> none  [from_behind(): return lax.ppermute(array, axis, pairs)]
    pallas_call x0 -> x1, Pallas kernels: none -> 135 us  [on_device(): pl.pallas_call(layer_kernel, out_shape=(out, out, out), in_specs=[pl.Bloc...]
    psum x1 -> x0, waiting for transfers between devices: 110 us -> none  [on_device(): lax.psum(pre_part.astype(jnp.bfloat16), 'exp').astype(jnp.float32)]
    add x64 -> x0, other arithmetic: 50.5 us -> none  [the longest x31 24.9 us: reverse_advance(): return from_behind(factor * incoming + local, 'ctx', -1)]
    all_to_all x2 -> x0, waiting for transfers between devices: 44.8 us -> none  [the longest x1 25.6 us: on_device(): lax.all_to_all(doubled(send_in), 'ctx', split_axis=0, concat_axis=0, tile...]
    dot_general x18 -> x0, matrix products: 44.7 us -> none  [the longest x2 19.5 us: contract_last(): lax.dot_general(left, right, (((1,), (1,)), ((), ())), preferred_element_...]
    all_to_all x1 -> x0, blocking collectives: 37.7 us -> none  [on_device(): lax.all_to_all(back_half, 'ctx', split_axis=0, concat_axis=0, tiled=True)]
  transfers between devices with their start and end apart: 65 -> 0, of which waited for: 65 -> 0; matrix products, arithmetic and copies ran while one was open for 1% -> 0% of each run, Pallas kernels for 0% -> 0%
where the time goes in v2:
time: 146 us; the launch traced here: 144 us
  Pallas kernels  135 us (92%)
  local copies, waits for them, and re-layouts  8.13 us (6%)
    pallas_call x1, Pallas kernels, on_device(): pl.pallas_call(layer_kernel, out_shape=(out, out, out), in_specs=[pl.Bloc...  135 us
    unnamed x5, local copies, waits for them, and re-layouts  8.13 us

profile of v2, /device:TPU:7, one launch (start us, length us, event | category | flops | bytes accessed | tf_op | source)
XLA Modules:
  0.0 144.2 jit_solution(10790554863918055795)
XLA Ops:
  0.6 1.4 copy.12.routes
  2.0 1.4 copy.13.gates
  3.5 135.5 %shard_map.112 = (bf16[128,1536]{1,0:T(8,128)(2,1)}, bf16[128,1536]{1,0:T(8,128)(2,1)}, bf16[128,1536]{1,0:T(8,128)(2,1)}) custom-call(f32[12]{0:T(128)} %rates.1, s32[128,2]{1,0:T(8,128)} %copy.12.routes, f32[128,2]{1,0:T(8,128)} %copy.13.gates, bf16[128,1536]{1,0:T(8,128)(2,1)} %queries.1, bf16[128,1536]{1,0:T(8,128)(2,1)} %keys.1, ...), custom_call_target="tpu_custom_call" | custom-call | tf_op jit(solution)/shard_map/pallas_call | solution.py:580
  138.9 1.8 %copy.17 = bf16[128,1536]{1,0:T(8,128)(2,1)} copy(bf16[128,1536]{1,0:T(8,128)(2,1)} %get-tuple-element.6) | data formatting | bytes 786432
  140.7 1.8 %copy.18 = bf16[128,1536]{1,0:T(8,128)(2,1)} copy(bf16[128,1536]{1,0:T(8,128)(2,1)} %get-tuple-element.7) | data formatting | bytes 786432
  142.5 1.8 %copy.19 = bf16[128,1536]{1,0:T(8,128)(2,1)} copy(bf16[128,1536]{1,0:T(8,128)(2,1)} %get-tuple-element.8) | data formatting | bytes 786432

commit v3 on v2

v3 whole, which is shorter than its diff:
```python
import jax
import jax.numpy as jnp
from jax import lax
from jax.experimental import pallas as pl
from jax.experimental.pallas import tpu as pltpu
from jax.sharding import PartitionSpec as P

DH = 128
MESH = pl.DeviceIdType.MESH
BF = jnp.bfloat16
F32 = jnp.float32
MID, FAR, NEAR = 0, 1, 2
CHUNKS = (6, 6, 4)
OFFSETS = (
    (3, 0), (1, 1), (1, 3), (3, 1), (3, 3), (0, 2),
    (2, 0), (1, 2), (3, 2), (2, 1), (2, 3), (2, 2),
    (0, 0), (0, 1), (0, 3), (1, 0),
)
OWN = OFFSETS.index((0, 0))
EXTRAS = FAR
MAIN = 16
EXTRA = 2
QUARTERS = 4


def nn(left, right):
    return lax.dot_general(left, right, (((1,), (0,)), ((), ())), preferred_element_type=F32)


def nt(left, right):
    return lax.dot_general(left, right, (((1,), (1,)), ((), ())), preferred_element_type=F32)


def tn(left, right):
    return lax.dot_general(left, right, (((0,), (0,)), ((), ())), preferred_element_type=F32)


def iota(shape, dim):
    return lax.broadcasted_iota(jnp.int32, shape, dim)


def each(lower, upper, action):
    def body(i, carry):
        action(i)
        return carry

    lax.fori_loop(lower, upper, body, 0)


def layer_kernel(
    rates_hbm, routes_hbm, gates_hbm, queries_hbm, keys_hbm, values_hbm, out_grad_hbm, up_hbm, down_hbm,
    query_out, key_out, value_out,
    query_g, key_g, value_g, rates, route_rows, gate_rows, queries, keys, values, out_grad, gates,
    up, down, main_hot, extra_hot, send_main, send_extra, rows_in, extra_in, partial,
    turned, below, above, slope, back, crossed, final, home_extra_out, home, home_extra,
    weights, intra, attn, local, entering, local_b, leaving, swap, summed, got, made, prefix, onward,
    swap_b, summed_b, got_b, made_b, prefix_b, onward_b, grad_out,
    key_part, value_part, faded_keys,
    load_sem, out_sem, main_s, main_r, relay_s, relay_r, extra_s, extra_r, hop_s, hop_r,
    fore_s, fore_r, rear_s, rear_r, reduce_s, reduce_r, gather_s, gather_r, cross_s, cross_r,
    home_s, home_r, homex_s, homex_r,
):
    block = queries.shape[0]
    group = queries.shape[1]
    heads = group // DH
    hidden = up.shape[1]
    half = hidden // 2
    quarter = group // QUARTERS
    scale = 1.0 / DH
    ctx = lax.axis_size("ctx")
    chips = ctx // 2
    me = lax.axis_index("ctx")
    level = lax.axis_index("exp")
    chip = lax.div(me, 2)
    core = lax.rem(me, 2)
    partner = me + 1 - 2 * core
    nxt, opp, prv = (lax.rem(level + i, 4) for i in (1, 2, 3))

    barrier = pltpu.get_barrier_semaphore()
    each(1, ctx, lambda k: pl.semaphore_signal(
        barrier, inc=1, device_id={"ctx": lax.rem(me + k, ctx)}, device_id_type=MESH))
    for peer in (nxt, prv):
        pl.semaphore_signal(barrier, inc=1, device_id={"exp": peer}, device_id_type=MESH)
    loads = [
        pltpu.make_async_copy(source, target, load_sem.at[i])
        for i, (source, target) in enumerate((
            (routes_hbm, route_rows), (out_grad_hbm, out_grad), (rates_hbm, rates), (keys_hbm, keys),
            (values_hbm, values), (queries_hbm, queries), (gates_hbm, gate_rows),
            (down_hbm.at[0], down), (up_hbm.at[0], up)))
    ]
    for load in loads:
        load.start()

    spans, base, short, first = [], 0, 0, 0
    for number, n in enumerate(CHUNKS):
        tall = 8 * n + (MAIN if number == EXTRAS else 0)
        spans.append((first, n, base, tall, short))
        first, base, short = first + n, base + 4 * tall, short + tall

    def block_row(k, side):
        number = sum(k >= first_k for first_k, *_ in spans) - 1
        first_k, n, start, tall, _ = spans[number]
        owner, place_in = divmod(k - first_k, n // 2)
        return pl.ds(pl.multiple_of(start + (2 * side + owner) * tall + place_in * MAIN, MAIN), MAIN)

    def chunk_slots(number):
        return range(spans[number][0], spans[number][0] + spans[number][1])

    loads[0].wait()
    diagonal = iota((block, block), 0) == iota((block, block), 1)

    def upright(row):
        return jnp.sum(jnp.where(diagonal, row, 0.0), axis=1, keepdims=True)

    routes = [upright(route_rows[k : k + 1, :].astype(F32)).astype(jnp.int32) for k in range(2)]
    expert = iota((block, chips), 1)
    hits = [(routes[k] == expert).astype(F32) for k in range(2)]
    earlier = (iota((block, block), 1) < iota((block, block), 0)).astype(BF)
    before = nn(earlier, (hits[0] + hits[1]).astype(BF))
    for k in range(2):
        placed = jnp.sum(before * hits[k], axis=1, keepdims=True).astype(jnp.int32)
        chosen = routes[k]
        target = jnp.where(placed < MAIN, chosen * MAIN + placed, -1)
        main_hot[k] = (target == iota((block, chips * MAIN), 1)).astype(F32).astype(BF)
        spare = jnp.where(placed >= MAIN, chosen * 8 + placed - MAIN, -64)
        for q in range(QUARTERS):
            extra_hot[k, q] = (spare + EXTRA * q == iota((block, chips * 8), 1)).astype(F32).astype(BF)

    def gather(a, source):
        pick = main_hot[0] + main_hot[1]

        def columns(i):
            cols = pl.ds(pl.multiple_of(i * 256, 256), 256)
            send_main[a, :, cols] = tn(pick, source[:, cols]).astype(BF)

        each(0, group // 256, columns)
        total = jnp.zeros((chips * 8, quarter), F32)
        for q in range(QUARTERS):
            total += tn(extra_hot[0, q] + extra_hot[1, q], source[:, q * quarter : (q + 1) * quarter])
        send_extra[a] = total.astype(BF).reshape(chips, 8, quarter)

    side_len = 4
    z, x = lax.div(chip, side_len), lax.rem(chip, side_len)

    def to_chip(k):
        dz, dx = OFFSETS[k]
        return lax.rem(z + dz, side_len) * side_len + lax.rem(x + dx, side_len)

    def from_chip(k):
        dz, dx = OFFSETS[k]
        return (lax.rem(z + side_len - dz, side_len) * side_len + lax.rem(x + side_len - dx, side_len)) * 2 + core

    def slot_rows(number):
        return pl.ds(pl.multiple_of(number * MAIN, MAIN), MAIN)

    def dispatch(a, k):
        return pltpu.make_async_remote_copy(
            src_ref=send_main.at[a, slot_rows(to_chip(k)), :], dst_ref=rows_in.at[a, block_row(k, core), :],
            send_sem=main_s.at[a], recv_sem=main_r.at[a, k],
            device_id={"ctx": to_chip(k) * 2 + core}, device_id_type=MESH)

    def relay(a, k, number):
        rows = rows_in.at[a, block_row(k, core), :]
        return pltpu.make_async_remote_copy(
            src_ref=rows, dst_ref=rows, send_sem=relay_s.at[a, number], recv_sem=relay_r.at[a, number],
            device_id={"ctx": partner}, device_id_type=MESH)

    def relay_all(a, number):
        rows = rows_in.at[a, pl.ds(spans[number][2], spans[number][1] * MAIN), :]
        return pltpu.make_async_remote_copy(
            src_ref=rows, dst_ref=rows, send_sem=relay_s.at[a, number], recv_sem=relay_r.at[a, number],
            device_id={"ctx": partner}, device_id_type=MESH)

    def dispatch_extra(a, k):
        return pltpu.make_async_remote_copy(
            src_ref=send_extra.at[a, to_chip(k)], dst_ref=extra_in.at[a, core * chips + k],
            send_sem=extra_s.at[a], recv_sem=extra_r.at[a],
            device_id={"ctx": to_chip(k) * 2 + core}, device_id_type=MESH)

    def dispatch_extra_all(a):
        return pltpu.make_async_remote_copy(
            src_ref=send_extra.at[a, pl.ds(0, chips - 1)], dst_ref=extra_in.at[a, pl.ds(0, chips - 1)],
            send_sem=extra_s.at[a], recv_sem=extra_r.at[a],
            device_id={"ctx": partner}, device_id_type=MESH)

    def relay_extra(a):
        rows = extra_in.at[a, pl.ds(core * chips, chips)]
        return pltpu.make_async_remote_copy(
            src_ref=rows, dst_ref=rows, send_sem=hop_s.at[a], recv_sem=hop_r.at[a],
            device_id={"ctx": partner}, device_id_type=MESH)

    def send_rows(a, number):
        if number == EXTRAS:
            for k in range(chips):
                if k != OWN:
                    dispatch_extra(a, k).start()
            extra_in[a, core * chips + OWN] = send_extra[a, chip]
        for k in chunk_slots(number):
            if k == OWN:
                rows_in[a, block_row(OWN, core), :] = send_main[a, slot_rows(chip), :]
                relay(a, OWN, number).start()
            else:
                dispatch(a, k).start()

    def pass_on(a, number):
        if number == EXTRAS:
            dispatch_extra_all(a).wait_recv()
            relay_extra(a).start()
        for k in chunk_slots(number):
            if k != OWN:
                dispatch(a, k).wait_recv()
                relay(a, k, number).start()

    def all_rows(a, number):
        _, _, start, tall, _ = spans[number]
        if number == EXTRAS:
            relay_extra(a).wait_recv()
            packed = extra_in[a].reshape(2 * chips * 8, quarter)
            count = 2 * chips * EXTRA
            row, col = iota((count, 2 * chips * 8), 0), iota((count, 2 * chips * 8), 1)
            origin = lax.div(row, 2) * 8 + lax.rem(row, 2)
            for q in range(QUARTERS):
                placed = nn((col == origin + EXTRA * q).astype(F32).astype(BF), packed).astype(BF)
                for owner in range(4):
                    at = start + owner * tall + tall - MAIN
                    rows_in[a, at : at + MAIN, q * quarter : (q + 1) * quarter] = placed[owner * MAIN : (owner + 1) * MAIN]
        relay_all(a, number).wait_recv()

    def expert_in(a, number):
        start, tall = spans[number][2:4]
        span = slice(start, start + 4 * tall)

        def block_of(at, wide):
            rows = rows_in[a, span, :]
            if a == 0:
                product = nt(rows, down[pl.ds(at, wide), :])
            else:
                product = nn(rows, up[:, pl.ds(at, wide)])
            partial[a, span, pl.ds(at, wide)] = product.astype(BF)

        for side, moves in enumerate((("turn_up", "own_down"), ("turn_down", "own_up"))):
            each(0, half // 256, lambda i: block_of(pl.multiple_of(side * half + i * 256, 128), 256))
            done = half // 256 * 256
            if done < half:
                block_of(side * half + done, half - done)
            for which in moves:
                reducer(a, number, which).start()

    low, high = pl.ds(0, half), pl.ds(half, half)

    def reducer(a, number, which):
        _, _, start, tall, rest = spans[number]

        def owned(by):
            return pl.ds(pl.multiple_of(start + by * tall, MAIN), tall)

        there = pl.ds(rest, tall)
        src, dst, peer = {
            "turn_up": ((owned(opp), low), (turned, 0, low), nxt),
            "turn_down": ((owned(opp), high), (turned, 0, high), prv),
            "own_up": ((owned(nxt), high), (below, 0, high), nxt),
            "own_down": ((owned(prv), low), (above, 0, low), prv),
            "sum_up": ((owned(nxt), low), (below, 0, low), nxt),
            "sum_down": ((owned(prv), high), (above, 0, high), prv),
        }[which]
        slot = ("turn_up", "turn_down", "own_up", "own_down", "sum_up", "sum_down").index(which)
        return pltpu.make_async_remote_copy(
            src_ref=partial.at[a, src[0], src[1]], dst_ref=dst[0].at[a, there, dst[2]],
            send_sem=reduce_s.at[a, number, slot], recv_sem=reduce_r.at[a, number, slot],
            device_id={"exp": peer}, device_id_type=MESH)

    def reduce_turn(a, number):
        _, _, start, tall, rest = spans[number]
        wide = half // 3
        for turn, onward, by, offset in (("turn_up", "sum_up", nxt, 0), ("turn_down", "sum_down", prv, half)):
            reducer(a, number, turn).wait_recv()
            rows = pl.ds(pl.multiple_of(start + by * tall, MAIN), tall)

            def columns(i):
                cols = pl.ds(pl.multiple_of(offset + i * wide, 128), wide)
                mine = partial[a, rows, cols].astype(F32) + turned[a, rest : rest + tall, cols].astype(F32)
                partial[a, rows, cols] = mine.astype(BF)

            each(0, 3, columns)
            reducer(a, number, onward).start()

    def finish(number):
        _, _, start, tall, rest = spans[number]
        for a in range(2):
            for which in ("own_up", "own_down", "sum_up", "sum_down"):
                reducer(a, number, which).wait_recv()
        rows = pl.ds(pl.multiple_of(start + level * tall, MAIN), tall)
        there = pl.ds(rest, tall)

        def columns(i):
            cols = pl.ds(pl.multiple_of(i * 384, 128), 384)

            def total(a):
                return (partial[a, rows, cols].astype(F32) + below[a, there, cols].astype(F32)
                        + above[a, there, cols].astype(F32))

            pre = total(1)
            sigma = jax.nn.sigmoid(pre)
            slope[rows, cols] = (total(0) * (sigma * (1.0 + pre * (1.0 - sigma)))).astype(BF)

        each(0, hidden // 384, columns)
        for which in ("up_low", "down_high", "up_high", "down_low"):
            spread(number, which).start()

    def spread(number, which):
        _, _, start, tall, _ = spans[number]

        def owned(by):
            return pl.ds(pl.multiple_of(start + by * tall, MAIN), tall)

        owner, cols, peer = {
            "up_low": (level, low, nxt),
            "up_high": (level, high, nxt),
            "down_high": (level, high, prv),
            "down_low": (level, low, prv),
            "on_up": (prv, low, nxt),
            "on_down": (nxt, high, prv),
        }[which]
        slot = ("up_low", "up_high", "down_high", "down_low", "on_up", "on_down").index(which)
        rows = slope.at[owned(owner), cols]
        return pltpu.make_async_remote_copy(
            src_ref=rows, dst_ref=rows,
            send_sem=gather_s.at[number, slot], recv_sem=gather_r.at[number, slot],
            device_id={"exp": peer}, device_id_type=MESH)

    def spread_on(number):
        spread(number, "up_low").wait_recv()
        spread(number, "on_up").start()
        spread(number, "down_high").wait_recv()
        spread(number, "on_down").start()

    def spread_done(number):
        for which in ("up_high", "down_low", "on_up", "on_down"):
            spread(number, which).wait_recv()

    def cross(number, side, piece):
        _, _, start, tall, rest = spans[number]
        cols = pl.ds(piece * (group // 2), group // 2)
        return pltpu.make_async_remote_copy(
            src_ref=back.at[pl.ds(pl.multiple_of(start + side * 2 * tall, MAIN), 2 * tall), cols],
            dst_ref=crossed.at[pl.ds(2 * rest, 2 * tall), cols],
            send_sem=cross_s.at[number, piece], recv_sem=cross_r.at[number, piece],
            device_id={"ctx": partner}, device_id_type=MESH)

    def expert_back(number, pieces_of=(0, 1)):
        _, _, start, tall, _ = spans[number]

        def columns(i):
            at = pl.multiple_of(i * 256, 256)
            product = nt(slope[start : start + 4 * tall, :], up[pl.ds(at, 256), :])
            back[start : start + 4 * tall, pl.ds(at, 256)] = product.astype(BF)

        for piece in pieces_of:
            each(piece * 3, piece * 3 + 3, columns)
            cross(number, 1 - core, piece).start()

    def go_home(k):
        number = sum(k >= first_k for first_k, *_ in spans) - 1
        first_k, n, _, tall, rest = spans[number]
        owner, place_in = divmod(k - first_k, n // 2)
        row = 2 * rest + owner * tall + place_in * MAIN
        return pltpu.make_async_remote_copy(
            src_ref=final.at[pl.ds(row, MAIN), :], dst_ref=home.at[slot_rows(chip), :],
            send_sem=home_s.at[0], recv_sem=home_r.at[0],
            device_id={"ctx": from_chip(k)}, device_id_type=MESH)

    def home_all():
        rows = pl.ds(0, (chips - 1) * MAIN)
        return pltpu.make_async_remote_copy(
            src_ref=final.at[rows, :], dst_ref=home.at[rows, :], send_sem=home_s.at[0], recv_sem=home_r.at[0],
            device_id={"ctx": partner}, device_id_type=MESH)

    def extra_home(k):
        return pltpu.make_async_remote_copy(
            src_ref=home_extra_out.at[k], dst_ref=home_extra.at[chip],
            send_sem=homex_s.at[0], recv_sem=homex_r.at[0],
            device_id={"ctx": from_chip(k)}, device_id_type=MESH)

    def extra_home_all():
        rows = pl.ds(0, chips - 1)
        return pltpu.make_async_remote_copy(
            src_ref=home_extra_out.at[rows], dst_ref=home_extra.at[rows],
            send_sem=homex_s.at[0], recv_sem=homex_r.at[0],
            device_id={"ctx": partner}, device_id_type=MESH)

    def return_rows(number):
        first_k, n, start, tall, rest = spans[number]
        own = pl.multiple_of(start + core * 2 * tall, MAIN)
        for piece in range(2):
            cross(number, core, piece).wait_recv()

            def columns(i):
                cols = pl.ds(pl.multiple_of(i * 256, 256), 256)
                mine = back[pl.ds(own, 2 * tall), cols].astype(F32)
                mine += crossed[2 * rest : 2 * rest + 2 * tall, cols].astype(F32)
                final[2 * rest : 2 * rest + 2 * tall, cols] = mine.astype(BF)

            each(piece * 3, piece * 3 + 3, columns)
        if number == EXTRAS:
            count = chips * EXTRA
            row, col = iota((chips * 8, count), 1), iota((chips * 8, count), 0)
            origin = lax.div(row, 2) * 8 + lax.rem(row, 2)
            total = jnp.zeros((chips * 8, quarter), F32)
            for q in range(QUARTERS):
                cols = slice(q * quarter, (q + 1) * quarter)
                spare = jnp.concatenate(
                    [final[2 * rest + (o + 1) * tall - MAIN : 2 * rest + (o + 1) * tall, cols] for o in range(2)], axis=0)
                total += nn((col == origin + EXTRA * q).astype(F32).astype(BF), spare)
            home_extra_out[...] = total.astype(BF).reshape(chips, 8, quarter)
            for k in range(chips):
                if k != OWN:
                    extra_home(k).start()
            home_extra[chip] = home_extra_out[OWN]
        for k in chunk_slots(number):
            if k != OWN:
                go_home(k).start()
            else:
                owner, place_in = divmod(k - first_k, n // 2)
                row = 2 * rest + owner * tall + place_in * MAIN
                home[slot_rows(chip), :] = final[row : row + MAIN, :]

    part = heads * DH // 2
    pieces = part // chips
    half_mine = pl.ds(pl.multiple_of(core * part, MAIN), part)
    half_other = pl.ds(pl.multiple_of((1 - core) * part, MAIN), part)

    class Scan:
        def __init__(self, reverse, own, result, swap, summed, got, made, prefix, onward, send, recv):
            self.reverse, self.own, self.result = reverse, own, result
            self.swap, self.summed, self.got, self.made = swap, summed, got, made
            self.prefix, self.onward, self.send, self.recv = prefix, onward, send, recv
            self.leads = core == (1 if reverse else 0)

        def trade(self):
            return pltpu.make_async_remote_copy(
                src_ref=self.own.at[half_other, :], dst_ref=self.swap, send_sem=self.send.at[0], recv_sem=self.recv.at[0],
                device_id={"ctx": partner}, device_id_type=MESH)

        def piece(self, number):
            return pl.ds(pl.multiple_of(number * pieces, MAIN), pieces)

        def out(self, stage, k):
            peer = lax.rem(chip + k, chips)
            source, target = ((self.summed, self.got), (self.made, self.prefix))[stage]
            return pltpu.make_async_remote_copy(
                src_ref=source.at[self.piece(peer), :], dst_ref=target.at[self.piece(chip), :],
                send_sem=self.send.at[1 + stage], recv_sem=self.recv.at[1 + stage],
                device_id={"ctx": peer * 2 + core}, device_id_type=MESH)

        def whole(self, stage):
            source, target = ((self.summed, self.got), (self.made, self.prefix))[stage]
            rows = pl.ds(0, (chips - 1) * pieces)
            return pltpu.make_async_remote_copy(
                src_ref=source.at[rows, :], dst_ref=target.at[rows, :],
                send_sem=self.send.at[1 + stage], recv_sem=self.recv.at[1 + stage],
                device_id={"ctx": partner}, device_id_type=MESH)

        def hand(self):
            return pltpu.make_async_remote_copy(
                src_ref=self.onward, dst_ref=self.result.at[half_mine, :], send_sem=self.send.at[3], recv_sem=self.recv.at[3],
                device_id={"ctx": partner}, device_id_type=MESH)

        def lead_rows(self, j):
            rows = pl.ds(j * DH, DH)
            own = self.own[pl.ds(pl.multiple_of(core * part + j * DH, DH), DH), :].astype(F32)
            other = self.swap[rows, :].astype(F32)
            fade = jnp.exp(jnp.full((DH, DH), -rates[core * (heads // 2) + j] * float(block), F32))
            first_one = jnp.where(self.leads, own, other)
            return rows, own, other, fade, first_one

        def join(self):
            self.trade().wait_recv()
            for j in range(heads // 2):
                rows, own, other, fade, first_one = self.lead_rows(j)
                self.summed[rows, :] = (fade * first_one + jnp.where(self.leads, other, own)).astype(BF)
            each(1, chips, lambda k: self.out(0, k).start())
            self.got[self.piece(chip), :] = self.summed[self.piece(chip), :]

        def run(self):
            row = iota((pieces, DH), 0) + chip * pieces
            rate = jnp.zeros((pieces, DH), F32)
            for j in range(heads // 2):
                rate = jnp.where((row >= j * DH) & (row < (j + 1) * DH), rates[core * (heads // 2) + j], rate)
            factor = jnp.exp(-rate * float(2 * block))
            self.whole(0).wait_recv()
            total = jnp.zeros((pieces, DH), F32)
            for i in range(chips):
                c = chips - 1 - i if self.reverse else i
                self.made[c * pieces : (c + 1) * pieces, :] = total.astype(BF)
                total = factor * total + self.got[c * pieces : (c + 1) * pieces, :].astype(F32)
            each(1, chips, lambda k: self.out(1, k).start())
            self.prefix[self.piece(chip), :] = self.made[self.piece(chip), :]

        def split(self):
            self.whole(1).wait_recv()
            for j in range(heads // 2):
                rows, _, _, fade, first_one = self.lead_rows(j)
                here = self.prefix[rows, :].astype(F32)
                after = fade * here + first_one
                self.onward[rows, :] = jnp.where(self.leads, after, here).astype(BF)
                target = pl.ds(pl.multiple_of(core * part + j * DH, DH), DH)
                self.result[target, :] = jnp.where(self.leads, here, after).astype(BF)
            self.hand().start()

        def done(self):
            self.hand().wait_recv()

        def sent(self):
            self.trade().wait_send()
            self.whole(0).wait_send()
            self.whole(1).wait_send()
            self.hand().wait_send()

    fore = Scan(False, local, entering, swap, summed, got, made, prefix, onward, fore_s, fore_r)
    rear = Scan(True, local_b, leaving, swap_b, summed_b, got_b, made_b, prefix_b, onward_b, rear_s, rear_r)
    place = iota((block, DH), 0).astype(F32)

    def write_out(i):
        source, target = ((query_g, query_out), (key_g, key_out), (value_g, value_out))[i]
        return pltpu.make_async_copy(source, target, out_sem.at[i])

    def head_cols(h):
        return slice(h * DH, (h + 1) * DH)

    def scan_trade(path):
        path.trade().start()

    def scan_join(path):
        path.join()

    def scan_run(path):
        path.run()

    def scan_split(path):
        path.split()

    def scan_done(path):
        path.done()

    def within(h):
        distance = (iota((block, block), 0) - iota((block, block), 1)).astype(F32)
        return jnp.where(distance >= 0.0, jnp.exp(-rates[h] * jnp.maximum(distance, 0.0)), 0.0)

    loads[1].wait()
    gather(0, out_grad)
    for i in (2, 3, 4):
        loads[i].wait()
    for h in range(heads):
        faded = (keys[:, head_cols(h)].astype(F32) * jnp.exp(-rates[h] * (float(block) - place))).astype(BF)
        local[h * DH : (h + 1) * DH, :] = tn(faded, values[:, head_cols(h)]).astype(BF)
    pl.semaphore_wait(barrier, ctx - 1 + 2)
    scan_trade(fore)
    send_rows(0, MID)
    for i in (5, 6):
        loads[i].wait()
    for k in range(2):
        gates[:, k : k + 1] = upright(gate_rows[k : k + 1, :])

    def inside(h):
        score = nt(queries[:, head_cols(h)], keys[:, head_cols(h)])
        weight = (scale * score * within(h)).astype(BF)
        weights[h] = weight
        intra[:, head_cols(h)] = nn(weight, values[:, head_cols(h)])

    for h in range(heads // 2):
        inside(h)
    scan_join(fore)
    for h in range(heads // 2, heads):
        inside(h)
    send_rows(0, NEAR)
    pass_on(0, MID)
    scan_run(fore)
    send_rows(0, FAR)
    all_rows(0, MID)
    loads[7].wait()
    expert_in(0, MID)
    pass_on(0, NEAR)
    scan_split(fore)
    all_rows(0, NEAR)
    scan_done(fore)
    for h in range(heads):
        across = nn(queries[:, head_cols(h)], entering[h * DH : (h + 1) * DH, :])
        total = intra[:, head_cols(h)] + scale * jnp.exp(-rates[h] * place) * across
        attn[:, head_cols(h)] = total.astype(BF)
    gather(1, attn)
    send_rows(1, FAR)
    send_rows(1, MID)
    send_rows(1, NEAR)
    reduce_turn(0, MID)
    expert_in(0, NEAR)
    pass_on(0, FAR)
    all_rows(0, FAR)
    expert_in(0, FAR)
    reduce_turn(0, NEAR)
    pass_on(1, FAR)
    all_rows(1, FAR)
    loads[8].wait()
    expert_in(1, FAR)
    reduce_turn(0, FAR)
    pass_on(1, MID)
    all_rows(1, MID)
    expert_in(1, MID)
    pass_on(1, NEAR)
    reduce_turn(1, FAR)
    all_rows(1, NEAR)
    expert_in(1, NEAR)
    reduce_turn(1, MID)
    finish(FAR)
    reduce_turn(1, NEAR)
    spread_on(FAR)
    finish(MID)
    spread_done(FAR)
    spread_on(MID)
    finish(NEAR)
    expert_back(FAR)
    return_rows(FAR)
    spread_done(MID)
    expert_back(MID, (0,))
    spread_on(NEAR)
    expert_back(MID, (1,))
    return_rows(MID)
    for a in range(2):
        dispatch_extra_all(a).wait_send()
        relay_extra(a).wait_send()
        sent = send_main.at[a, pl.ds(0, (chips - 1) * MAIN), :]
        pltpu.make_async_remote_copy(
            src_ref=sent, dst_ref=sent, send_sem=main_s.at[a], recv_sem=main_r.at[a, 0],
            device_id={"ctx": partner}, device_id_type=MESH).wait_send()
        for number in range(len(CHUNKS)):
            relay_all(a, number).wait_send()
            for which in ("turn_up", "turn_down", "own_up", "own_down", "sum_up", "sum_down"):
                reducer(a, number, which).wait_send()
    fore.sent()
    spread_done(NEAR)
    expert_back(NEAR)
    return_rows(NEAR)

    extra_home_all().wait_recv()
    home_all().wait_recv()
    for q in range(QUARTERS):
        cols = slice(q * quarter, (q + 1) * quarter)
        total = out_grad[:, cols].astype(F32)
        for k in range(2):
            mine = nn(main_hot[k], home[:, cols])
            mine += nn(extra_hot[k, q], home_extra[...].reshape(chips * 8, quarter))
            total += gates[:, k : k + 1] * mine
        grad_out[:, cols] = total.astype(BF)
    for h in range(heads):
        faded = (queries[:, head_cols(h)].astype(F32) * jnp.exp(-rates[h] * (place + 1.0))).astype(BF)
        local_b[h * DH : (h + 1) * DH, :] = tn(faded, grad_out[:, head_cols(h)]).astype(BF)
    scan_trade(rear)
    for h in range(heads):
        if h == heads // 3:
            scan_join(rear)
        cols = head_cols(h)
        grad = grad_out[:, cols]
        dweight = (scale * nt(grad, values[:, cols]) * within(h)).astype(BF)
        across = nt(grad, entering[h * DH : (h + 1) * DH, :])
        query_g[:, cols] = (nn(dweight, keys[:, cols]) + scale * jnp.exp(-rates[h] * place) * across).astype(BF)
        key_part[:, cols] = tn(dweight, queries[:, cols])
        value_part[:, cols] = tn(weights[h], grad)
    write_out(0).start()
    scan_run(rear)
    extra_home_all().wait_send()
    home_all().wait_send()
    for number in range(len(CHUNKS)):
        for piece in range(2):
            cross(number, 1 - core, piece).wait_send()
        for which in ("up_low", "up_high", "down_high", "down_low", "on_up", "on_down"):
            spread(number, which).wait_send()
    for h in range(heads):
        cols = head_cols(h)
        fade = scale * jnp.exp(-rates[h] * (float(block) - 1.0 - place))
        attn[:, cols] = (fade * values[:, cols].astype(F32)).astype(BF)
        faded_keys[:, cols] = (fade * keys[:, cols].astype(F32)).astype(BF)
    scan_split(rear)
    scan_done(rear)
    for h in range(heads):
        cols = head_cols(h)
        state = leaving[h * DH : (h + 1) * DH, :]
        key_g[:, cols] = (key_part[:, cols] + nt(attn[:, cols], state)).astype(BF)
    write_out(1).start()
    for h in range(heads):
        cols = head_cols(h)
        state = leaving[h * DH : (h + 1) * DH, :]
        value_g[:, cols] = (value_part[:, cols] + nn(faded_keys[:, cols], state)).astype(BF)
    write_out(2).start()
    for i in range(3):
        write_out(i).wait()

    rear.sent()


def leave_kernel(first, second, third, first_out, second_out, third_out, held, sems):
    sources, targets = (first, second, third), (first_out, second_out, third_out)
    inward = [pltpu.make_async_copy(sources[i], held.at[i], sems.at[0, i]) for i in range(3)]
    outward = [pltpu.make_async_copy(held.at[i], targets[i], sems.at[1, i]) for i in range(3)]
    for copy in inward:
        copy.start()
    for before, after in zip(inward, outward):
        before.wait()
        after.start()
    for copy in outward:
        copy.wait()


def on_device(
    queries, keys, values, out_grad, up_weight, down_weight, decay_rates, routes, gate_weights
):
    block, group = queries.shape
    heads = group // DH
    hidden = up_weight.shape[2]
    ctx = lax.axis_size("ctx")
    chips = ctx // 2
    slots = chips * MAIN
    total = 2 * chips * (MAIN + EXTRA)
    quarter = group // QUARTERS
    count = len(CHUNKS)
    state = (heads * DH, DH)
    dma = pltpu.SemaphoreType.DMA
    raw = pl.BlockSpec(memory_space=pl.ANY)
    out = jax.ShapeDtypeStruct((block, group), BF)
    grads = pl.pallas_call(
        layer_kernel,
        out_shape=(out, out, out),
        in_specs=[raw] * 9,
        out_specs=(raw, raw, raw),
        scratch_shapes=[pltpu.VMEM((block, group), BF)] * 3
        + [
            pltpu.SMEM((heads,), F32),
            pltpu.VMEM((2, block), jnp.int32),
            pltpu.VMEM((2, block), F32),
        ]
        + [pltpu.VMEM((block, group), BF)] * 4
        + [
            pltpu.VMEM((block, 2), F32),
            pltpu.VMEM((group, hidden), BF),
            pltpu.VMEM((hidden, group), BF),
            pltpu.VMEM((2, block, slots), BF),
            pltpu.VMEM((2, QUARTERS, block, chips * 8), BF),
            pltpu.VMEM((2, slots, group), BF),
            pltpu.VMEM((2, chips, 8, quarter), BF),
            pltpu.VMEM((2, total, group), BF),
            pltpu.VMEM((2, 2 * chips, 8, quarter), BF),
            pltpu.VMEM((2, total, hidden), BF),
            pltpu.VMEM((2, total // 4, hidden), BF),
            pltpu.VMEM((2, total // 4, hidden), BF),
            pltpu.VMEM((2, total // 4, hidden), BF),
            pltpu.VMEM((total, hidden), BF),
            pltpu.VMEM((total, group), BF),
            pltpu.VMEM((total // 2, group), BF),
            pltpu.VMEM((total // 2, group), BF),
            pltpu.VMEM((chips, 8, quarter), BF),
            pltpu.VMEM((slots, group), BF),
            pltpu.VMEM((chips, 8, quarter), BF),
            pltpu.VMEM((heads, block, block), BF),
            pltpu.VMEM((block, group), F32),
            pltpu.VMEM((block, group), BF),
        ]
        + [pltpu.VMEM(state, BF)] * 4
        + [pltpu.VMEM((heads * DH // 2, DH), BF)] * 12
        + [
            pltpu.VMEM((block, group), BF),
            pltpu.VMEM((block, group), F32),
            pltpu.VMEM((block, group), F32),
            pltpu.VMEM((block, group), BF),
            dma((9,)), dma((3,)),
            dma((2,)), dma((2, chips)),
            dma((2, count)), dma((2, count)),
        ]
        + [dma((2,))] * 4
        + [dma((4,))] * 4
        + [dma((2, count, 6))] * 2
        + [dma((count, 6))] * 2
        + [dma((count, 2))] * 2
        + [dma((1,))] * 4,
        compiler_params=pltpu.CompilerParams(
            collective_id=0, has_side_effects=True, vmem_limit_bytes=67043328
        ),
    )(decay_rates, routes.T, gate_weights.T, queries, keys, values, out_grad, up_weight, down_weight)
    return pl.pallas_call(
        leave_kernel,
        out_shape=(out, out, out),
        in_specs=[raw] * 3,
        out_specs=(raw, raw, raw),
        scratch_shapes=[pltpu.VMEM((3, block, group), BF), dma((2, 3))],
    )(*grads)


def solution(mesh):
    placed = (
        P("ctx", "exp"),
        P("ctx", "exp"),
        P("ctx", "exp"),
        P("ctx", "exp"),
        P("ctx", "exp", None),
        P("ctx", None, "exp"),
        P("exp"),
        P("ctx", None),
        P("ctx", None),
    )
    return jax.shard_map(
        on_device,
        mesh=mesh,
        in_specs=placed,
        out_specs=(P("ctx", "exp"), P("ctx", "exp"), P("ctx", "exp")),
        check_vma=False,
    )
```

time: 146 us -> 123 us (0.84)
  Pallas kernels: 135 us -> 121 us
  local copies, waits for them, and re-layouts: 8.13 us -> 0 us
    pallas_call x1 -> x2, Pallas kernels: 135 us -> 121 us  [the longest x1 119 us: on_device(): pl.pallas_call(layer_kernel, out_shape=(out, out, out), in_specs=[raw] *...]
    unnamed x5 -> x0, local copies, waits for them, and re-layouts: 8.13 us -> none
where the time goes in v3:
time: 123 us; the launch traced here: 122 us
  Pallas kernels  121 us (98%)
    pallas_call x1, Pallas kernels, on_device(): pl.pallas_call(layer_kernel, out_shape=(out, out, out), in_specs=[raw] *...  119 us

profile of v3, /device:TPU:7, one launch (start us, length us, event | category | flops | bytes accessed | tf_op | source)
XLA Modules:
  0.0 121.7 jit_solution(452999560293055746)
XLA Ops:
  0.6 119.0 %shard_map.112 = (bf16[128,1536]{1,0:T(8,128)(2,1)}, bf16[128,1536]{1,0:T(8,128)(2,1)}, bf16[128,1536]{1,0:T(8,128)(2,1)}) custom-call(f32[12]{0:T(128)} %rates_hbm.1, s32[2,128]{1,0:T(2,128)} %bitcast.2, f32[2,128]{1,0:T(2,128)} %bitcast.3, bf16[128,1536]{1,0:T(8,128)(2,1)} %queries_hbm.1, bf16[128,1536]{1,0:T(8,128)(2,1)} %keys_hbm.1, ...), custom_call_target="tpu_custom_call" | custom-call | tf_op jit(solution)/shard_map/pallas_call | solution.py:728
  119.7 2.1 %shard_map.113 = (bf16[128,1536]{1,0:T(8,128)(2,1)}, bf16[128,1536]{1,0:T(8,128)(2,1)}, bf16[128,1536]{1,0:T(8,128)(2,1)}) custom-call(bf16[128,1536]{1,0:T(8,128)(2,1)} %get-tuple-element.6.first, bf16[128,1536]{1,0:T(8,128)(2,1)} %get-tuple-element.7.second, bf16[128,1536]{1,0:T(8,128)(2,1)} %get-tuple-element.8.third), custom_call_target="tpu_custom_call" | custom-call | tf_op jit(solution)/shard_map/pallas_call | solution.py:786

commit v4 on v3

--- a/solution.py
+++ b/solution.py
@@ -51,7 +51,7 @@
     rates_hbm, routes_hbm, gates_hbm, queries_hbm, keys_hbm, values_hbm, out_grad_hbm, up_hbm, down_hbm,
     query_out, key_out, value_out,
     query_g, key_g, value_g, rates, route_rows, gate_rows, queries, keys, values, out_grad, gates,
-    up, down, main_hot, extra_hot, send_main, send_extra, rows_in, extra_in, partial,
+    up, down, main_hot, extra_hot, main_pick, extra_pick, send_main, send_extra, rows_in, extra_in, partial,
     turned, below, above, slope, back, crossed, final, home_extra_out, home, home_extra,
     weights, intra, attn, local, entering, local_b, leaving, swap, summed, got, made, prefix, onward,
     swap_b, summed_b, got_b, made_b, prefix_b, onward_b, grad_out,
@@ -126,17 +126,20 @@
         for q in range(QUARTERS):
             extra_hot[k, q] = (spare + EXTRA * q == iota((block, chips * 8), 1)).astype(F32).astype(BF)
 
+    unit = diagonal.astype(F32).astype(BF)
+    main_pick[...] = tn(main_hot[0] + main_hot[1], unit).astype(BF)
+    for q in range(QUARTERS):
+        extra_pick[q] = tn(extra_hot[0, q] + extra_hot[1, q], unit).astype(BF)
+
     def gather(a, source):
-        pick = main_hot[0] + main_hot[1]
-
         def columns(i):
             cols = pl.ds(pl.multiple_of(i * 256, 256), 256)
-            send_main[a, :, cols] = tn(pick, source[:, cols]).astype(BF)
+            send_main[a, :, cols] = nn(main_pick[...], source[:, cols]).astype(BF)
 
         each(0, group // 256, columns)
         total = jnp.zeros((chips * 8, quarter), F32)
         for q in range(QUARTERS):
-            total += tn(extra_hot[0, q] + extra_hot[1, q], source[:, q * quarter : (q + 1) * quarter])
+            total += nn(extra_pick[q], source[:, q * quarter : (q + 1) * quarter])
         send_extra[a] = total.astype(BF).reshape(chips, 8, quarter)
 
     side_len = 4
@@ -555,7 +558,6 @@
         local[h * DH : (h + 1) * DH, :] = tn(faded, values[:, head_cols(h)]).astype(BF)
     pl.semaphore_wait(barrier, ctx - 1 + 2)
     scan_trade(fore)
-    send_rows(0, MID)
     for i in (5, 6):
         loads[i].wait()
     for k in range(2):
@@ -570,11 +572,12 @@
     for h in range(heads // 2):
         inside(h)
     scan_join(fore)
+    send_rows(0, MID)
     for h in range(heads // 2, heads):
         inside(h)
+    scan_run(fore)
     send_rows(0, NEAR)
     pass_on(0, MID)
-    scan_run(fore)
     send_rows(0, FAR)
     all_rows(0, MID)
     loads[7].wait()
@@ -696,16 +699,14 @@
     rear.sent()
 
 
-def leave_kernel(first, second, third, first_out, second_out, third_out, held, sems):
-    sources, targets = (first, second, third), (first_out, second_out, third_out)
-    inward = [pltpu.make_async_copy(sources[i], held.at[i], sems.at[0, i]) for i in range(3)]
-    outward = [pltpu.make_async_copy(held.at[i], targets[i], sems.at[1, i]) for i in range(3)]
-    for copy in inward:
+def leave_kernel(first, second, third, first_out, second_out, third_out, sems):
+    copies = [
+        pltpu.make_async_copy(source, target, sems.at[i])
+        for i, (source, target) in enumerate(((first, first_out), (second, second_out), (third, third_out)))
+    ]
+    for copy in copies:
         copy.start()
-    for before, after in zip(inward, outward):
-        before.wait()
-        after.start()
-    for copy in outward:
+    for copy in copies:
         copy.wait()
 
 
@@ -724,6 +725,7 @@
     state = (heads * DH, DH)
     dma = pltpu.SemaphoreType.DMA
     raw = pl.BlockSpec(memory_space=pl.ANY)
+    kept = pl.BlockSpec(memory_space=pltpu.HBM)
     out = jax.ShapeDtypeStruct((block, group), BF)
     grads = pl.pallas_call(
         layer_kernel,
@@ -743,6 +745,8 @@
             pltpu.VMEM((hidden, group), BF),
             pltpu.VMEM((2, block, slots), BF),
             pltpu.VMEM((2, QUARTERS, block, chips * 8), BF),
+            pltpu.VMEM((slots, block), BF),
+            pltpu.VMEM((QUARTERS, chips * 8, block), BF),
             pltpu.VMEM((2, slots, group), BF),
             pltpu.VMEM((2, chips, 8, quarter), BF),
             pltpu.VMEM((2, total, group), BF),
@@ -780,15 +784,16 @@
         + [dma((count, 2))] * 2
         + [dma((1,))] * 4,
         compiler_params=pltpu.CompilerParams(
-            collective_id=0, has_side_effects=True, vmem_limit_bytes=67043328
+            collective_id=0, has_side_effects=True, vmem_limit_bytes=52 << 20
         ),
     )(decay_rates, routes.T, gate_weights.T, queries, keys, values, out_grad, up_weight, down_weight)
     return pl.pallas_call(
         leave_kernel,
         out_shape=(out, out, out),
         in_specs=[raw] * 3,
-        out_specs=(raw, raw, raw),
-        scratch_shapes=[pltpu.VMEM((3, block, group), BF), dma((2, 3))],
+        out_specs=(kept, kept, kept),
+        scratch_shapes=[dma((3,))],
+        compiler_params=pltpu.CompilerParams(vmem_limit_bytes=1 << 20),
     )(*grads)
 
 

time: 123 us -> 124 us (level)
  Pallas kernels: 121 us -> 117 us
  local copies, waits for them, and re-layouts: 0 us -> 4 us
    unnamed x0 -> x10, local copies, waits for them, and re-layouts: none -> 4 us
    pallas_call x1, Pallas kernels: 119 us -> 116 us  [on_device(): pl.pallas_call(layer_kernel, out_shape=(out, out, out), in_specs=[raw] *...]
where the time goes in v4:
time: 124 us; the launch traced here: 122 us
  Pallas kernels  117 us (94%)
  local copies, waits for them, and re-layouts  4 us (3%)
    pallas_call x1, Pallas kernels, on_device(): pl.pallas_call(layer_kernel, out_shape=(out, out, out), in_specs=[raw] *...  116 us
    unnamed x10, local copies, waits for them, and re-layouts  4 us

profile of v4, /device:TPU:7, one launch (start us, length us, event | category | flops | bytes accessed | tf_op | source)
XLA Modules:
  0.0 121.9 jit_solution(7767632883898262473)
XLA Ops:
  0.6 0.0 copy-start
  0.6 1.0 copy-done
  1.6 0.0 copy-start.1
  1.6 1.0 copy-done.1
  2.6 0.0 copy-start.2
  2.6 0.7 copy-done.2
  3.3 0.0 copy-start.3
  3.3 0.7 copy-done.3
  4.0 0.0 copy-start.4
  4.0 0.7 copy-done.4
  4.6 116.2 %shard_map.112 = (bf16[128,1536]{1,0:T(8,128)(2,1)S(1)}, bf16[128,1536]{1,0:T(8,128)(2,1)S(1)}, bf16[128,1536]{1,0:T(8,128)(2,1)S(1)}) custom-call(f32[12]{0:T(128)S(1)} %copy-done.4, s32[2,128]{1,0:T(2,128)S(1)} %bitcast.2, f32[2,128]{1,0:T(2,128)S(1)} %bitcast.3, bf16[128,1536]{1,0:T(8,128)(2,1)S(1)} %copy-done, bf16[128,1536]{1,0:T(8,128)(2,1)S(1)} %copy-done.1, ...), custom_call_target="tpu_custom_call" | custom-call | tf_op jit(solution)/shard_map/pallas_call | solution.py:730
  120.9 1.0 shard_map.113
Async XLA Ops:
  0.6 1.0 copy-start
  1.6 1.0 copy-start.1
  2.6 0.7 copy-start.2
  3.3 0.7 copy-start.3
  4.0 0.7 copy-start.4

commit v5 on v4

--- a/solution.py
+++ b/solution.py
@@ -784,7 +784,7 @@
         + [dma((count, 2))] * 2
         + [dma((1,))] * 4,
         compiler_params=pltpu.CompilerParams(
-            collective_id=0, has_side_effects=True, vmem_limit_bytes=52 << 20
+            collective_id=0, has_side_effects=True, vmem_limit_bytes=55250000
         ),
     )(decay_rates, routes.T, gate_weights.T, queries, keys, values, out_grad, up_weight, down_weight)
     return pl.pallas_call(

time: 124 us -> 122 us (0.984)
  local copies, waits for them, and re-layouts: 4 us -> 2.01 us
    unnamed x10 -> x6, local copies, waits for them, and re-layouts: 4 us -> 2.01 us
where the time goes in v5:
time: 122 us; the launch traced here: 120 us
  Pallas kernels  117 us (96%)
  local copies, waits for them, and re-layouts  2.01 us (2%)
    pallas_call x1, Pallas kernels, on_device(): pl.pallas_call(layer_kernel, out_shape=(out, out, out), in_specs=[raw] *...  116 us

profile of v5, /device:TPU:7, one launch (start us, length us, event | category | flops | bytes accessed | tf_op | source)
XLA Modules:
  0.0 119.9 jit_solution(14134858267605405870)
XLA Ops:
  0.6 0.0 copy-start
  0.6 0.7 copy-done
  1.3 0.0 copy-start.1
  1.3 0.7 copy-done.1
  2.0 0.0 copy-start.2
  2.0 0.7 copy-done.2
  2.6 116.2 %shard_map.112 = (bf16[128,1536]{1,0:T(8,128)(2,1)S(1)}, bf16[128,1536]{1,0:T(8,128)(2,1)S(1)}, bf16[128,1536]{1,0:T(8,128)(2,1)S(1)}) custom-call(f32[12]{0:T(128)S(1)} %copy-done.2, s32[2,128]{1,0:T(2,128)S(1)} %bitcast.2, f32[2,128]{1,0:T(2,128)S(1)} %bitcast.3, bf16[128,1536]{1,0:T(8,128)(2,1)} %queries_hbm.1, bf16[128,1536]{1,0:T(8,128)(2,1)} %keys_hbm.1, ...), custom_call_target="tpu_custom_call" | custom-call | tf_op jit(solution)/shard_map/pallas_call | solution.py:730
  118.9 1.0 shard_map.113
Async XLA Ops:
  0.6 0.7 copy-start
  1.3 0.7 copy-start.1
  2.0 0.7 copy-start.2
